TPU v7x, 256 devices: a whole 4x4x8 slice. The times are simulated.
256 devices in a mesh: pair: 8 (over x, core), grow: 4 (over y), gcol: 8 (over z).
Axes of the slice: x: 4, y: 4, z: 8, core: 2. Of those that a mesh axis runs over, the one named last changes fastest.
Arguments:
- core_matrix: bfloat16 [12288, 12288], P('grow', 'gcol'), may hold values from -0.00048828125 to 0.00048828125
- pair_panels: bfloat16 [48, 32, 12288], P('pair', None, ('grow', 'gcol')), may hold values from -6 to 6
- amplitudes: bfloat16 [48, 32, 32], P('pair'), may hold values from -0.1875 to 0.1875
- pair_widths: int32 [48], P('pair'), may hold values from 8 to 32
- batch_plan: int32 [48], P('pair'), may hold values from 0 to 47, each once
Outputs:
- residual: float32 [48, 1024], P('pair', ('grow', 'gcol'))
Inputs may be any that keep to these rules, and one draw needn't show every extreme that they name: batch_plan names every pair exactly once.
All inputs are finite; a program needn't handle non-finite values.
Results may differ from a plain program's by a relative error of at most 0.015.
Values may be sent and summed in bfloat16 or wider, within the bound.
No kernel may reach another device: no remote copies, remote signals or barrier semaphores. Data moves between devices by JAX's collectives and lax.ppermute only.
A program may use at most 64 MiB of HBM per device.

v0:
```python
import jax
import jax.numpy as jnp
from jax import lax
from jax.sharding import PartitionSpec as P


def laid_out(blocks, dim):
    blocks = jnp.moveaxis(blocks, 0, dim)
    dims = blocks.shape
    return blocks.reshape(*dims[:dim], dims[dim] * dims[dim + 1], *dims[dim + 2 :])


def gather_in_order(x, axes, order):
    blocks = x[None]
    for k in order:
        blocks = lax.all_gather(blocks, axes[k], axis=0, tiled=True)
    current = [lax.axis_size(axes[k]) for k in reversed(order)]
    blocks = blocks.reshape(*current, *x.shape)
    turned = sorted(range(len(order)), key=lambda place: order[len(order) - 1 - place])
    return blocks.transpose(*turned, *range(len(order), blocks.ndim)).reshape(-1, *x.shape)


def gathered_by_axis(x, axes, order, dim):
    return laid_out(gather_in_order(x, axes, order), dim)


def cut_along(x, dim, length):
    dims = x.shape
    blocks = x.reshape(*dims[:dim], length, dims[dim] // length, *dims[dim + 1 :])
    return jnp.moveaxis(blocks, dim, 0)


def sent_and_summed(x, axis, dim):
    blocks = cut_along(x, dim, lax.axis_size(axis))
    arrived = lax.all_to_all(blocks, axis, split_axis=0, concat_axis=0, tiled=True)
    return arrived.sum(axis=0)


def copy_for_each(x, axis):
    copies = jnp.broadcast_to(x, (lax.axis_size(axis), *x.shape))
    return lax.all_to_all(copies, axis, split_axis=0, concat_axis=0, tiled=True)


def gather_directly(x, axis, dim):
    return laid_out(copy_for_each(x, axis), dim)


def local(core_matrix, pair_panels, amplitudes, pair_widths, batch_plan):
    depth = amplitudes.shape[1]
    live = (
        lax.broadcasted_iota(jnp.int32, (pair_widths.shape[0], depth), 1) < pair_widths[:, None]
    ).astype(jnp.bfloat16)
    masked = amplitudes * live[:, :, None] * live[:, None, :]
    row_index = lax.axis_index("grow")
    col_index = lax.axis_index("gcol")
    row_len = core_matrix.shape[0]
    col_len = core_matrix.shape[1]
    gathered = gathered_by_axis(pair_panels, ("grow", "gcol"), (0, 1), 2)
    left = lax.dynamic_slice_in_dim(gathered, row_index * row_len, row_len, 2)
    right = lax.dynamic_slice_in_dim(gathered, col_index * col_len, col_len, 2)

    def slot_term(items):
        left_panel, right_panel, amps, mask = items
        projected = jnp.dot(amps, right_panel, preferred_element_type=jnp.float32).astype(
            jnp.bfloat16
        )
        coupled = lax.dot_general(
            left_panel, projected, (((0,), (0,)), ((), ())), preferred_element_type=jnp.float32
        ).astype(jnp.bfloat16)
        coupled = lax.optimization_barrier(coupled)
        weighted = (core_matrix.astype(jnp.float32) * coupled.astype(jnp.float32)).astype(
            jnp.bfloat16
        )
        back = lax.dot_general(
            weighted, right_panel, (((1,), (1,)), ((), ())), preferred_element_type=jnp.float32
        ).astype(jnp.bfloat16)
        partial_sum = jnp.dot(left_panel, back, preferred_element_type=jnp.float32)
        keep = mask.astype(jnp.float32)
        return (partial_sum * keep[:, None] * keep[None, :]).reshape(depth * depth)

    terms = lax.map(slot_term, (left, right, masked, live))
    reduced = sent_and_summed(terms, ("grow", "gcol"), 1)
    every_row = gather_directly(reduced, "pair", 0)
    return jnp.take(every_row, batch_plan, axis=0)


def solution(mesh):
    in_specs = (
        P("grow", "gcol"),
        P("pair", None, ("grow", "gcol")),
        P("pair", None, None),
        P("pair"),
        P("pair"),
    )
    out_specs = P("pair", ("grow", "gcol"))
    return jax.shard_map(local, mesh=mesh, in_specs=in_specs, out_specs=out_specs, check_vma=False)
```

profile of v0, /device:TPU:1, one launch (start us, length us, event | category | flops | bytes accessed | tf_op | source)
XLA Modules:
  0.0 216.1 jit_solution(8615705036225841198)
XLA Ops:
  6.5 14.1 %all-gather = bf16[24,32,384]{2,1,0:T(8,128)(2,1)} all-gather(bf16[6,32,384]{2,1,0:T(8,128)(2,1)} %param.8), channel_id=2, replica_groups=mesh['pair'=8,'grow'=4,'gcol'=8] {'grow'}, dimensions={0}, use_global_device_ids=true | all-gather | bytes 737280 | tf_op jit(solution)/shard_map/all_gather | solution.py:16
  20.7 0.7 compare_select_fusion
  21.3 0.7 fusion.27
  22.0 0.9 multiply_multiply_fusion
  22.9 61.9 %all-gather.3.cloned.1.call-done = bf16[32,6,32,384]{3,2,1,0:T(8,128)(2,1)} async-done(((bf16[4,6,32,384]{3,2,1,0:T(8,128)(2,1)}), bf16[32,6,32,384]{3,2,1,0:T(8,128)(2,1)}) %all-gather.3.cloned.1.call-update) | async-done | bytes 4718608 | tf_op jit(solution)/shard_map/all_gather | solution.py:16
  84.9 2.8 %copy.9 = bf16[4,8,6,32,384]{4,3,2,1,0:T(8,128)(2,1)S(1)} copy(bf16[4,8,6,32,384]{4,3,2,0,1:T(8,128)(2,1)} %bitcast.46) | data formatting | bytes 9437184 | tf_op jit(solution)/shard_map/transpose | solution.py:20
  87.7 0.8 copy.12
  88.5 0.1 constant_dynamic-slice_fusion.2
  88.7 89.0 %while.10 = (s32[]{:T(128)}, f32[6,1024]{1,0:T(8,128)S(1)}, bf16[6,32,3072]{2,1,0:T(8,128)(2,1)S(1)}, bf16[3072,1536]{1,0:T(8,128)(2,1)}, bf16[6,32,32]{2,1,0:T(...) while((s32[]{:T(128)}, f32[6,1024]{1,0:T(8,128)S(1)}, ...), condition=%wide.region_1.2_spmd, body=%wide.region_0.1_spmd.sunk | while | flops 637159424 | bytes 28933924 | solution.py:81
  88.7 5.2 %convolution_convert_fusion.3 = bf16[3072,1536]{1,0:T(8,128)(2,1)} fusion(bf16[6,32,3072]{2,1,0:T(8,128)(2,1)S(1)} %get-tuple-element.120, s32[]{:T(128)} %get-tuple-element.109, bf16[6,32,1536]{2,1,0:T(8,128)(2,1)S(1)} %get-tuple-element.123, bf16[6,32,32]{2,1,0:T(8,128)(2,1)S(1)} %get-tuple-element.122), kind=kOutput, calls=%fused_computation.2.clone.1 | convolution fusion | flops 309903360 | bytes 9741824 | tf_op jit(solution)/shard_map/while/body/eval_jaxpr/dot_general | solution.py:67
  93.9 9.4 %fusion.41 = f32[32,32]{1,0:T(8,128)S(1)} fusion(bf16[3072,1536]{1,0:T(8,128)(2,1)} %convolution_convert_fusion.3, bf16[3072,1536]{1,0:T(8,128)(2,1)} %get-tuple-element.121, bf16[6,32,3072]{2,1,0:T(8,128)(2,1)S(1)} %get-tuple-element.120, s32[]{:T(128)} %get-tuple-element.109, bf16[6,32,1536]{2,1,0:T(8,128)(2,1)S(1)} %get-tuple-element.123, ...), kind=kOutput, calls=%fused_computation.8.clone.1 | convolution fusion | flops 327256064 | bytes 19175424 | tf_op jit(solution)/shard_map/while/body/eval_jaxpr/dot_general | solution.py:77
  103.3 0.1 broadcast_in_dim.39
  103.4 0.1 dynamic_update_slice.5
  103.6 5.2 %convolution_convert_fusion.3 = bf16[3072,1536]{1,0:T(8,128)(2,1)} fusion(bf16[6,32,3072]{2,1,0:T(8,128)(2,1)S(1)} %get-tuple-element.120, s32[]{:T(128)} %get-tuple-element.109, bf16[6,32,1536]{2,1,0:T(8,128)(2,1)S(1)} %get-tuple-element.123, bf16[6,32,32]{2,1,0:T(8,128)(2,1)S(1)} %get-tuple-element.122), kind=kOutput, calls=%fused_computation.2.clone.1 | convolution fusion | flops 309903360 | bytes 9741824 | tf_op jit(solution)/shard_map/while/body/eval_jaxpr/dot_general | solution.py:67
  108.7 9.4 %fusion.41 = f32[32,32]{1,0:T(8,128)S(1)} fusion(bf16[3072,1536]{1,0:T(8,128)(2,1)} %convolution_convert_fusion.3, bf16[3072,1536]{1,0:T(8,128)(2,1)} %get-tuple-element.121, bf16[6,32,3072]{2,1,0:T(8,128)(2,1)S(1)} %get-tuple-element.120, s32[]{:T(128)} %get-tuple-element.109, bf16[6,32,1536]{2,1,0:T(8,128)(2,1)S(1)} %get-tuple-element.123, ...), kind=kOutput, calls=%fused_computation.8.clone.1 | convolution fusion | flops 327256064 | bytes 19175424 | tf_op jit(solution)/shard_map/while/body/eval_jaxpr/dot_general | solution.py:77
  118.2 0.1 broadcast_in_dim.39
  118.3 0.1 dynamic_update_slice.5
  118.4 5.2 %convolution_convert_fusion.3 = bf16[3072,1536]{1,0:T(8,128)(2,1)} fusion(bf16[6,32,3072]{2,1,0:T(8,128)(2,1)S(1)} %get-tuple-element.120, s32[]{:T(128)} %get-tuple-element.109, bf16[6,32,1536]{2,1,0:T(8,128)(2,1)S(1)} %get-tuple-element.123, bf16[6,32,32]{2,1,0:T(8,128)(2,1)S(1)} %get-tuple-element.122), kind=kOutput, calls=%fused_computation.2.clone.1 | convolution fusion | flops 309903360 | bytes 9741824 | tf_op jit(solution)/shard_map/while/body/eval_jaxpr/dot_general | solution.py:67
  123.6 9.4 %fusion.41 = f32[32,32]{1,0:T(8,128)S(1)} fusion(bf16[3072,1536]{1,0:T(8,128)(2,1)} %convolution_convert_fusion.3, bf16[3072,1536]{1,0:T(8,128)(2,1)} %get-tuple-element.121, bf16[6,32,3072]{2,1,0:T(8,128)(2,1)S(1)} %get-tuple-element.120, s32[]{:T(128)} %get-tuple-element.109, bf16[6,32,1536]{2,1,0:T(8,128)(2,1)S(1)} %get-tuple-element.123, ...), kind=kOutput, calls=%fused_computation.8.clone.1 | convolution fusion | flops 327256064 | bytes 19175424 | tf_op jit(solution)/shard_map/while/body/eval_jaxpr/dot_general | solution.py:77
  133.0 0.1 broadcast_in_dim.39
  133.1 0.1 dynamic_update_slice.5
  133.2 5.2 %convolution_convert_fusion.3 = bf16[3072,1536]{1,0:T(8,128)(2,1)} fusion(bf16[6,32,3072]{2,1,0:T(8,128)(2,1)S(1)} %get-tuple-element.120, s32[]{:T(128)} %get-tuple-element.109, bf16[6,32,1536]{2,1,0:T(8,128)(2,1)S(1)} %get-tuple-element.123, bf16[6,32,32]{2,1,0:T(8,128)(2,1)S(1)} %get-tuple-element.122), kind=kOutput, calls=%fused_computation.2.clone.1 | convolution fusion | flops 309903360 | bytes 9741824 | tf_op jit(solution)/shard_map/while/body/eval_jaxpr/dot_general | solution.py:67
  138.4 9.4 %fusion.41 = f32[32,32]{1,0:T(8,128)S(1)} fusion(bf16[3072,1536]{1,0:T(8,128)(2,1)} %convolution_convert_fusion.3, bf16[3072,1536]{1,0:T(8,128)(2,1)} %get-tuple-element.121, bf16[6,32,3072]{2,1,0:T(8,128)(2,1)S(1)} %get-tuple-element.120, s32[]{:T(128)} %get-tuple-element.109, bf16[6,32,1536]{2,1,0:T(8,128)(2,1)S(1)} %get-tuple-element.123, ...), kind=kOutput, calls=%fused_computation.8.clone.1 | convolution fusion | flops 327256064 | bytes 19175424 | tf_op jit(solution)/shard_map/while/body/eval_jaxpr/dot_general | solution.py:77
  147.8 0.1 broadcast_in_dim.39
  148.0 0.1 dynamic_update_slice.5
  148.1 5.2 %convolution_convert_fusion.3 = bf16[3072,1536]{1,0:T(8,128)(2,1)} fusion(bf16[6,32,3072]{2,1,0:T(8,128)(2,1)S(1)} %get-tuple-element.120, s32[]{:T(128)} %get-tuple-element.109, bf16[6,32,1536]{2,1,0:T(8,128)(2,1)S(1)} %get-tuple-element.123, bf16[6,32,32]{2,1,0:T(8,128)(2,1)S(1)} %get-tuple-element.122), kind=kOutput, calls=%fused_computation.2.clone.1 | convolution fusion | flops 309903360 | bytes 9741824 | tf_op jit(solution)/shard_map/while/body/eval_jaxpr/dot_general | solution.py:67
  153.2 9.4 %fusion.41 = f32[32,32]{1,0:T(8,128)S(1)} fusion(bf16[3072,1536]{1,0:T(8,128)(2,1)} %convolution_convert_fusion.3, bf16[3072,1536]{1,0:T(8,128)(2,1)} %get-tuple-element.121, bf16[6,32,3072]{2,1,0:T(8,128)(2,1)S(1)} %get-tuple-element.120, s32[]{:T(128)} %get-tuple-element.109, bf16[6,32,1536]{2,1,0:T(8,128)(2,1)S(1)} %get-tuple-element.123, ...), kind=kOutput, calls=%fused_computation.8.clone.1 | convolution fusion | flops 327256064 | bytes 19175424 | tf_op jit(solution)/shard_map/while/body/eval_jaxpr/dot_general | solution.py:77
  162.7 0.1 broadcast_in_dim.39
  162.8 0.1 dynamic_update_slice.5
  162.9 5.2 %convolution_convert_fusion.3 = bf16[3072,1536]{1,0:T(8,128)(2,1)} fusion(bf16[6,32,3072]{2,1,0:T(8,128)(2,1)S(1)} %get-tuple-element.120, s32[]{:T(128)} %get-tuple-element.109, bf16[6,32,1536]{2,1,0:T(8,128)(2,1)S(1)} %get-tuple-element.123, bf16[6,32,32]{2,1,0:T(8,128)(2,1)S(1)} %get-tuple-element.122), kind=kOutput, calls=%fused_computation.2.clone.1 | convolution fusion | flops 309903360 | bytes 9741824 | tf_op jit(solution)/shard_map/while/body/eval_jaxpr/dot_general | solution.py:67
  168.1 9.4 %fusion.41 = f32[32,32]{1,0:T(8,128)S(1)} fusion(bf16[3072,1536]{1,0:T(8,128)(2,1)} %convolution_convert_fusion.3, bf16[3072,1536]{1,0:T(8,128)(2,1)} %get-tuple-element.121, bf16[6,32,3072]{2,1,0:T(8,128)(2,1)S(1)} %get-tuple-element.120, s32[]{:T(128)} %get-tuple-element.109, bf16[6,32,1536]{2,1,0:T(8,128)(2,1)S(1)} %get-tuple-element.123, ...), kind=kOutput, calls=%fused_computation.8.clone.1 | convolution fusion | flops 327256064 | bytes 19175424 | tf_op jit(solution)/shard_map/while/body/eval_jaxpr/dot_general | solution.py:77
  177.5 0.1 broadcast_in_dim.39
  177.6 0.1 dynamic_update_slice.5
  177.7 0.1 reshape.66
  177.8 0.1 copy.11
  177.9 0.7 reshape.79
  178.6 6.9 %all-to-all-start = ((f32[32,1,192]{2,1,0:T(1,128)}), f32[32,1,192]{2,1,0:T(1,128)S(1)}, u32[]{:S(2)}, u32[]{:S(2)}) async-start(f32[32,1,192]{2,1,0:T(1,128)} %reshape.79), calls=%async_computation | async-start | bytes 65536 | tf_op jit(solution)/shard_map/all_to_all | solution.py:35
  185.5 8.7 %all-to-all-done = f32[32,1,192]{2,1,0:T(1,128)S(1)} async-done(((f32[32,1,192]{2,1,0:T(1,128)}), f32[32,1,192]{2,1,0:T(1,128)S(1)}, u32[]{:S(2)}, u32[]{:S(2)}) %all-to-all-start) | async-done | bytes 24608 | tf_op jit(solution)/shard_map/all_to_all | solution.py:35
  194.3 0.5 broadcast.34
  194.8 0.7 reduce
  195.5 0.1 reshape.80
  195.6 0.7 reshape.81
  196.3 6.4 %all-to-all-start.1 = ((f32[8,1,192]{2,1,0:T(1,128)}), f32[8,1,192]{2,1,0:T(1,128)S(1)}, u32[]{:S(2)}, u32[]{:S(2)}) async-start(f32[8,1,192]{2,1,0:T(1,128)} %reshape.81), calls=%async_computation.1 | async-start | bytes 16384 | tf_op jit(solution)/shard_map/all_to_all | solution.py:41
  202.7 4.6 %all-to-all-done.1 = f32[8,1,192]{2,1,0:T(1,128)S(1)} async-done(((f32[8,1,192]{2,1,0:T(1,128)}), f32[8,1,192]{2,1,0:T(1,128)S(1)}, u32[]{:S(2)}, u32[]{:S(2)}) %all-to-all-start.1) | async-done | bytes 6176 | tf_op jit(solution)/shard_map/all_to_all | solution.py:41
  207.3 0.7 reduce.1
  208.0 0.1 reshape.82
  208.0 0.6 gather_fusion
  208.6 0.7 broadcast_select_fusion
  (17 shorter events, 0.2 us)
Async XLA Ops:
  6.5 78.3 %all-gather.3.cloned.1.call-start = ((), (), s32[]{:S(2)}) async-start(), calls=%async_computation.2 | async-start | bytes 5308416 | tf_op jit(solution)/shard_map/all_gather | solution.py:16
  88.7 96.8 %copy-start = (s32[6]{0:T(128)S(1)}, s32[6]{0:T(128)}, u32[]{:S(2)}) copy-start(s32[6]{0:T(128)} %param.11) | copy-start | bytes 76
  178.6 15.6 %all-to-all-start = ((f32[32,1,192]{2,1,0:T(1,128)}), f32[32,1,192]{2,1,0:T(1,128)S(1)}, u32[]{:S(2)}, u32[]{:S(2)}) async-start(f32[32,1,192]{2,1,0:T(1,128)} %reshape.79), calls=%async_computation | async-start | bytes 65536 | tf_op jit(solution)/shard_map/all_to_all | solution.py:35
  196.3 11.0 %all-to-all-start.1 = ((f32[8,1,192]{2,1,0:T(1,128)}), f32[8,1,192]{2,1,0:T(1,128)S(1)}, u32[]{:S(2)}, u32[]{:S(2)}) async-start(f32[8,1,192]{2,1,0:T(1,128)} %reshape.81), calls=%async_computation.1 | async-start | bytes 16384 | tf_op jit(solution)/shard_map/all_to_all | solution.py:41
Sparse Core Ops, SparseCore 0:
  20.8 64.0 all-gather.2
where the time goes:
time: 217 us; the launch traced here: 216 us
  matrix products  87.6 us (40%)
  waiting for transfers between devices  75.3 us (35%)
  blocking collectives  14.1 us (6%)
  between operations  13.5 us (6%)
  starting transfers between devices  13.2 us (6%)
  local copies, waits for them, and re-layouts  7.84 us (4%)
  other arithmetic  4.41 us (2%)
    all_gather x1, waiting for transfers between devices, gather_in_order(): blocks = lax.all_gather(blocks, axes[k], axis=0, tiled=True)  61.9 us
    dot_general x6, matrix products, slot_term(): partial_sum = jnp.dot(left_panel, back, preferred_element_type=jnp.float32)  56.6 us
    dot_general x6, matrix products, slot_term(): lax.dot_general(left_panel, projected, (((0,), (0,)), ((), ())), preferre...  31 us
    all_gather x1, blocking collectives, gather_in_order(): blocks = lax.all_gather(blocks, axes[k], axis=0, tiled=True)  14.1 us
    all_to_all x1, waiting for transfers between devices, sent_and_summed(): lax.all_to_all(blocks, axis, split_axis=0, concat_axis=0, tiled=True)  8.74 us
    all_to_all x1, starting transfers between devices, sent_and_summed(): lax.all_to_all(blocks, axis, split_axis=0, concat_axis=0, tiled=True)  6.86 us
    all_to_all x1, starting transfers between devices, copy_for_each(): return lax.all_to_all(copies, axis, split_axis=0, concat_axis=0, tiled=True)  6.35 us
    all_to_all x1, waiting for transfers between devices, copy_for_each(): return lax.all_to_all(copies, axis, split_axis=0, concat_axis=0, tiled=True)  4.61 us
  transfers between devices with their start and end apart: 3, of which 3 were waited for; matrix products, arithmetic and copies ran while one was open for 1% of the time, Pallas kernels for 0%

commit v1 on v0

v1 whole, which is shorter than its diff:
```python
import jax
import jax.numpy as jnp
from jax import lax
from jax.experimental import pallas as pl
from jax.experimental.pallas import tpu as pltpu
from jax.sharding import PartitionSpec as P

F32 = jnp.float32
BF16 = jnp.bfloat16
NN = (((1,), (0,)), ((), ()))
NT = (((1,), (1,)), ((), ()))
TN = (((0,), (0,)), ((), ()))


def dot(a, b, dims):
    return lax.dot_general(a, b, dims, preferred_element_type=F32)


def shift(size, by):
    return [(i, (i + by) % size) for i in range(size)]


def ring_chunks(own, axis):
    size = lax.axis_size(axis)
    chunks, back = [own], [0]
    right = left = own
    for step in range(1, size // 2 + 1):
        right = lax.ppermute(right, axis, shift(size, 1))
        chunks.append(right)
        back.append(step)
        if step < size - step:
            left = lax.ppermute(left, axis, shift(size, -1))
            chunks.append(left)
            back.append(-step)
    return chunks, back


def column_chunks(own, rows, cols):
    per = rows
    pairs = [(per * j + g, g * cols + j) for g in range(rows) for j in range(cols)]
    first = lax.ppermute(own, ("grow", "gcol"), pairs)
    return [first] + [lax.ppermute(first, "grow", shift(rows, d)) for d in range(1, rows)]


def pair_kernel(place, core_ref, left_ref, r0, r1, r2, r3, amps_ref, live_ref, out_ref, right_ref, proj_ref):
    step, pair = pl.program_id(0), pl.program_id(1)
    chunk = left_ref.shape[-1]

    @pl.when((step == 0) & (pair == 0))
    def _():
        for d, ref in enumerate((r0, r1, r2, r3)):
            at = pl.multiple_of(lax.rem(place[0] + 4 - d, 4) * chunk, 128)
            right_ref[:, :, pl.ds(at, chunk)] = ref[...]

    @pl.when(step == 0)
    def _():
        proj_ref[pair] = dot(amps_ref[pair], right_ref[pair], NN).astype(BF16)
        out_ref[pair] = jnp.zeros(out_ref.shape[1:], F32)

    left = left_ref[0, 0]
    coupled = dot(left, proj_ref[pair], TN).astype(BF16)
    weighted = core_ref[...] * coupled
    back = dot(right_ref[pair], weighted, NT).astype(BF16)
    out_ref[pair] += dot(left, back, NT)

    @pl.when(step == pl.num_programs(0) - 1)
    def _():
        out_ref[pair] = out_ref[pair] * live_ref[pair]


def local(core_matrix, pair_panels, amplitudes, pair_widths, batch_plan):
    pairs, depth, chunk = pair_panels.shape
    rows, cols = lax.axis_size("grow"), lax.axis_size("gcol")
    live = lax.broadcasted_iota(jnp.int32, (pairs, depth), 1) < pair_widths[:, None]
    live = live[:, :, None] & live[:, None, :]
    masked = jnp.where(live, amplitudes, 0)
    right = column_chunks(pair_panels, rows, cols)
    chunks, back = ring_chunks(pair_panels, "gcol")
    left = jnp.stack(chunks)
    origin = lax.rem(lax.axis_index("gcol") + cols - jnp.array(back, jnp.int32), cols)
    place = jnp.concatenate([lax.axis_index("grow")[None], origin])
    whole = pl.BlockSpec(memory_space=pltpu.VMEM)
    terms = pl.pallas_call(
        pair_kernel,
        out_shape=jax.ShapeDtypeStruct((pairs, depth, depth), F32),
        grid_spec=pltpu.PrefetchScalarGridSpec(
            num_scalar_prefetch=1,
            grid=(cols, pairs),
            in_specs=[
                pl.BlockSpec((chunk, core_matrix.shape[1]), lambda s, p, at: (at[1 + s], 0)),
                pl.BlockSpec((1, 1, depth, chunk), lambda s, p, at: (s, p, 0, 0)),
            ]
            + [whole] * 6,
            out_specs=whole,
            scratch_shapes=[
                pltpu.VMEM((pairs, depth, rows * chunk), BF16),
                pltpu.VMEM((pairs, depth, rows * chunk), BF16),
            ],
        ),
        compiler_params=pltpu.CompilerParams(vmem_limit_bytes=48 << 20),
    )(place, core_matrix, left, *right, masked, live.astype(F32))
    parts = terms.reshape(pairs, rows * cols, depth * depth // (rows * cols))
    parts = parts.transpose(1, 0, 2).reshape(rows * cols, -1)
    mine = lax.all_to_all(parts, ("grow", "gcol"), 0, 0, tiled=True).sum(axis=0)
    copies = jnp.broadcast_to(mine, (lax.axis_size("pair"), *mine.shape))
    every = lax.all_to_all(copies, "pair", 0, 0, tiled=True)
    return jnp.take(every.reshape(-1, depth * depth // (rows * cols)), batch_plan, axis=0)


def solution(mesh):
    in_specs = (
        P("grow", "gcol"),
        P("pair", None, ("grow", "gcol")),
        P("pair", None, None),
        P("pair"),
        P("pair"),
    )
    out_specs = P("pair", ("grow", "gcol"))
    return jax.shard_map(local, mesh=mesh, in_specs=in_specs, out_specs=out_specs, check_vma=False)
```

time: 217 us -> 129 us (0.59)
  matrix products: 87.6 us -> 0 us
  waiting for transfers between devices: 75.3 us -> 23 us
  Pallas kernels: 0 us -> 48.6 us
  starting transfers between devices: 13.2 us -> 49.5 us
  blocking collectives: 14.1 us -> 0 us
  between operations: 13.5 us -> 0.17 us
  local copies, waits for them, and re-layouts: 7.84 us -> 3.13 us
    dot_general x12 -> x0, matrix products: 87.6 us -> none  [the longest x6 56.6 us: slot_term(): partial_sum = jnp.dot(left_panel, back, preferred_element_type=jnp.float32)]
    all_gather x1 -> x0, waiting for transfers between devices: 61.9 us -> none  [gather_in_order(): blocks = lax.all_gather(blocks, axes[k], axis=0, tiled=True)]
    pallas_call x0 -> x1, Pallas kernels: none -> 48.6 us  [local(): pl.pallas_call(pair_kernel, out_shape=jax.ShapeDtypeStruct((pairs, depth,...]
    ppermute x0 -> x11, starting transfers between devices: none -> 32.2 us  [the longest x3 18.5 us: column_chunks(): lax.ppermute(first, 'grow', shift(rows, d))]
    all_gather x1 -> x0, blocking collectives: 14.1 us -> none  [gather_in_order(): blocks = lax.all_gather(blocks, axes[k], axis=0, tiled=True)]
    ppermute x0 -> x11, waiting for transfers between devices: none -> 9.63 us  [the longest x4 9.61 us: ring_chunks(): right = lax.ppermute(right, axis, shift(size, 1))]
    all_to_all x2, starting transfers between devices: 13.2 us -> 17.2 us  [the longest x1 10.7 us: local(): every = lax.all_to_all(copies, 'pair', 0, 0, tiled=True)]
    transpose x2 -> x1, local copies, waits for them, and re-layouts: 2.87 us -> 0.06 us  [local(): parts = parts.transpose(1, 0, 2).reshape(rows * cols, -1)]
  transfers between devices with their start and end apart: 3 -> 13, of which waited for: 3 -> 5; matrix products, arithmetic and copies ran while one was open for 1% -> 3% of each run, Pallas kernels for 0% -> 0%
where the time goes in v1:
time: 129 us; the launch traced here: 128 us
  starting transfers between devices  49.5 us (38%)
  Pallas kernels  48.6 us (38%)
  waiting for transfers between devices  23 us (18%)
  other arithmetic  3.87 us (3%)
  local copies, waits for them, and re-layouts  3.13 us (2%)
    pallas_call x1, Pallas kernels, local(): pl.pallas_call(pair_kernel, out_shape=jax.ShapeDtypeStruct((pairs, depth,...  48.6 us
    ppermute x3, starting transfers between devices, column_chunks(): lax.ppermute(first, 'grow', shift(rows, d))  18.5 us
    all_to_all x1, starting transfers between devices, local(): every = lax.all_to_all(copies, 'pair', 0, 0, tiled=True)  10.7 us
    ppermute x3, starting transfers between devices, ring_chunks(): left = lax.ppermute(left, axis, shift(size, -1))  9.73 us
    ppermute x4, waiting for transfers between devices, ring_chunks(): right = lax.ppermute(right, axis, shift(size, 1))  9.61 us
    all_to_all x1, waiting for transfers between devices, local(): mine = lax.all_to_all(parts, ('grow', 'gcol'), 0, 0, tiled=True).sum(axis=0)  8.74 us
    all_to_all x1, starting transfers between devices, local(): mine = lax.all_to_all(parts, ('grow', 'gcol'), 0, 0, tiled=True).sum(axis=0)  6.56 us
    all_to_all x1, waiting for transfers between devices, local(): every = lax.all_to_all(copies, 'pair', 0, 0, tiled=True)  4.6 us
  transfers between devices with their start and end apart: 13, of which 5 were waited for; matrix products, arithmetic and copies ran while one was open for 3% of the time, Pallas kernels for 0%

profile of v1, /device:TPU:1, one launch (start us, length us, event | category | flops | bytes accessed | tf_op | source)
XLA Modules:
  0.0 128.2 jit_solution(3301577426196795204)
XLA Ops:
  0.0 2.5 %collective-permute-start = (bf16[6,32,384]{2,1,0:T(8,128)(2,1)}, bf16[6,32,384]{2,1,0:T(8,128)(2,1)S(1)}, u32[]{:S(2)}, u32[]{:S(2)}) collective-permute-start(bf16[6,32,384]{2,1,0:T(8,128)(2,1)} %param.7), channel_id=1, source_target_pairs={{0,1},{1,2},{2,3},{3,4},{4,5},{5,6},{6,7},{7,0},{8,9},{9,10},{10,1... | collective-permute-start | bytes 442376 | tf_op jit(solution)/shard_map/ppermute | solution.py:28
  2.5 3.9 %collective-permute-start.1 = (bf16[6,32,384]{2,1,0:T(8,128)(2,1)}, bf16[6,32,384]{2,1,0:T(8,128)(2,1)S(1)}, u32[]{:S(2)}, u32[]{:S(2)}) collective-permute-start(bf16[6,32,384]{2,1,0:T(8,128)(2,1)} %param.7), channel_id=1, source_target_pairs={{0,7},{1,0},{2,1},{3,2},{4,3},{5,4},{6,5},{7,6},{8,15},{9,8},{10,9... | collective-permute-start | bytes 442376 | tf_op jit(solution)/shard_map/ppermute | solution.py:32
  6.4 1.6 %collective-permute-start.7 = (bf16[6,32,384]{2,1,0:T(8,128)(2,1)}, bf16[6,32,384]{2,1,0:T(8,128)(2,1)S(1)}, u32[]{:S(2)}, u32[]{:S(2)}) collective-permute-start(bf16[6,32,384]{2,1,0:T(8,128)(2,1)} %param.7), channel_id=1, source_target_pairs={{0,0},{4,1},{8,2},{12,3},{16,4},{20,5},{24,6},{28,7},{1,8},{5,9},{... | collective-permute-start | bytes 442376 | tf_op jit(solution)/shard_map/ppermute | solution.py:41
  8.0 0.9 bitcast_dynamic-update-slice_fusion.7
  8.9 0.7 iota_compare_fusion
  9.6 0.1 and_convert_fusion.live_ref
  9.7 0.9 and_select_fusion.amps_ref
  10.6 0.7 compare_select_fusion
  11.3 0.7 compare_select_fusion.1
  11.9 0.1 pad_add_fusion.place
  12.0 0.0 collective-permute-done.7.r0
  12.0 14.2 %collective-permute-start.10 = (bf16[6,32,384]{2,1,0:T(8,128)(2,1)S(1)}, bf16[6,32,384]{2,1,0:T(8,128)(2,1)S(1)}, u32[]{:S(2)}, u32[]{:S(2)}) collective-permute-start(bf16[6,32,384]{2,1,0:T(8,128)(2,1)S(1)} %collective-permute-done.7.r0), channel_id=1, source_target_pairs={{0,24},{8,0},{16,8},{24,16},{1,25},{9,1},{17,9},{25,17},{2,26},{10... | collective-permute-start | bytes 442376 | tf_op jit(solution)/shard_map/ppermute | solution.py:42
  26.3 0.0 collective-permute-start.8
  26.3 4.2 %collective-permute-start.9 = (bf16[6,32,384]{2,1,0:T(8,128)(2,1)S(1)}, bf16[6,32,384]{2,1,0:T(8,128)(2,1)S(1)}, u32[]{:S(2)}, u32[]{:S(2)}) collective-permute-start(bf16[6,32,384]{2,1,0:T(8,128)(2,1)S(1)} %collective-permute-done.7.r0), channel_id=1, source_target_pairs={{0,16},{8,24},{16,0},{24,8},{1,17},{9,25},{17,1},{25,9},{2,18},{10... | collective-permute-start | bytes 442376 | tf_op jit(solution)/shard_map/ppermute | solution.py:42
  30.5 0.0 collective-permute-done
  30.5 0.0 collective-permute-start.2
  30.5 0.0 collective-permute-done.1
  30.5 2.7 %collective-permute-start.3 = (bf16[6,32,384]{2,1,0:T(8,128)(2,1)S(1)}, bf16[6,32,384]{2,1,0:T(8,128)(2,1)S(1)}, u32[]{:S(2)}, u32[]{:S(2)}) collective-permute-start(bf16[6,32,384]{2,1,0:T(8,128)(2,1)S(1)} %collective-permute-done.1), channel_id=1, source_target_pairs={{0,7},{1,0},{2,1},{3,2},{4,3},{5,4},{6,5},{7,6},{8,15},{9,8},{10,9... | collective-permute-start | bytes 442376 | tf_op jit(solution)/shard_map/ppermute | solution.py:32
  33.3 2.4 %collective-permute-done.2 = bf16[6,32,384]{2,1,0:T(8,128)(2,1)S(1)} collective-permute-done((bf16[6,32,384]{2,1,0:T(8,128)(2,1)S(1)}, bf16[6,32,384]{2,1,0:T(8,128)(2,1)S(1)}, u32[]{:S(2)}, u32[]{:S(2)}) %collective-permute-start.2) | collective-permute-done | bytes 147488 | tf_op jit(solution)/shard_map/ppermute | solution.py:28
  35.7 0.0 collective-permute-start.4
  35.7 0.0 collective-permute-done.3
  35.7 3.0 %collective-permute-start.5 = (bf16[6,32,384]{2,1,0:T(8,128)(2,1)S(1)}, bf16[6,32,384]{2,1,0:T(8,128)(2,1)S(1)}, u32[]{:S(2)}, u32[]{:S(2)}) collective-permute-start(bf16[6,32,384]{2,1,0:T(8,128)(2,1)S(1)} %collective-permute-done.3), channel_id=1, source_target_pairs={{0,7},{1,0},{2,1},{3,2},{4,3},{5,4},{6,5},{7,6},{8,15},{9,8},{10,9... | collective-permute-start | bytes 442376 | tf_op jit(solution)/shard_map/ppermute | solution.py:32
  38.8 2.1 %collective-permute-done.4 = bf16[6,32,384]{2,1,0:T(8,128)(2,1)S(1)} collective-permute-done((bf16[6,32,384]{2,1,0:T(8,128)(2,1)S(1)}, bf16[6,32,384]{2,1,0:T(8,128)(2,1)S(1)}, u32[]{:S(2)}, u32[]{:S(2)}) %collective-permute-start.4) | collective-permute-done | bytes 147488 | tf_op jit(solution)/shard_map/ppermute | solution.py:28
  40.9 0.0 collective-permute-start.6
  40.9 0.0 collective-permute-done.5
  41.0 5.1 %collective-permute-done.6 = bf16[6,32,384]{2,1,0:T(8,128)(2,1)S(1)} collective-permute-done((bf16[6,32,384]{2,1,0:T(8,128)(2,1)S(1)}, bf16[6,32,384]{2,1,0:T(8,128)(2,1)S(1)}, u32[]{:S(2)}, u32[]{:S(2)}) %collective-permute-start.6) | collective-permute-done | bytes 147488 | tf_op jit(solution)/shard_map/ppermute | solution.py:28
  46.1 0.0 copy-start
  46.2 0.0 collective-permute-done.10.r3
  46.2 0.0 collective-permute-done.8.r1
  46.2 0.0 collective-permute-done.9.r2
  46.2 48.6 %shard_map.64 = f32[6,32,32]{2,1,0:T(8,128)S(1)} custom-call(s32[9]{0:T(128)S(1)} %pad_add_fusion.place, bf16[3072,1536]{1,0:T(8,128)(2,1)} %core_ref.1, bf16[8,6,32,384]{3,2,1,0:T(8,128)(2,1)S(1)} %bitcast_dynamic-update-slice_fusion.left_ref, bf16[6,32,384]{2,1,0:T(8,128)(2,1)S(1)} %collective-permute-done.7.r0, ...), custom_call_target="tpu_custom_call" | custom-call | tf_op jit(solution)/shard_map/pallas_call | solution.py:83
  94.8 0.1 copy.8
  94.8 0.7 all_to_all.13
  95.6 6.6 %all-to-all-start = ((f32[32,1,192]{2,1,0:T(1,128)}), f32[32,1,192]{2,1,0:T(1,128)S(1)}, u32[]{:S(2)}, u32[]{:S(2)}) async-start(f32[32,1,192]{2,1,0:T(1,128)} %all_to_all.13), calls=%async_computation | async-start | bytes 65536 | tf_op jit(solution)/shard_map/all_to_all | solution.py:104
  102.1 0.0 copy-done
  102.2 8.7 %all-to-all-done = f32[32,1,192]{2,1,0:T(1,128)S(1)} async-done(((f32[32,1,192]{2,1,0:T(1,128)}), f32[32,1,192]{2,1,0:T(1,128)S(1)}, u32[]{:S(2)}, u32[]{:S(2)}) %all-to-all-start) | async-done | bytes 24608 | tf_op jit(solution)/shard_map/all_to_all | solution.py:104
  110.9 0.1 reduce_sum.9
  111.0 0.6 broadcast_in_dim.28
  111.6 10.7 %all-to-all-start.1 = ((f32[8,1,192]{2,1,0:T(1,128)}), f32[8,1,192]{2,1,0:T(1,128)S(1)}, u32[]{:S(2)}, u32[]{:S(2)}) async-start(f32[8,1,192]{2,1,0:T(1,128)} %broadcast_in_dim.28), calls=%async_computation.1 | async-start | bytes 16384 | tf_op jit(solution)/shard_map/all_to_all | solution.py:106
  122.3 4.6 %all-to-all-done.1 = f32[8,1,192]{2,1,0:T(1,128)S(1)} async-done(((f32[8,1,192]{2,1,0:T(1,128)}), f32[8,1,192]{2,1,0:T(1,128)S(1)}, u32[]{:S(2)}, u32[]{:S(2)}) %all-to-all-start.1) | async-done | bytes 6176 | tf_op jit(solution)/shard_map/all_to_all | solution.py:106
  126.9 0.1 reshape.49
  127.0 0.6 gather_fusion
  127.5 0.7 broadcast_select_fusion
  (10 shorter events, 0.2 us)
Async XLA Ops:
  0.0 30.5 %collective-permute-start = (bf16[6,32,384]{2,1,0:T(8,128)(2,1)}, bf16[6,32,384]{2,1,0:T(8,128)(2,1)S(1)}, u32[]{:S(2)}, u32[]{:S(2)}) collective-permute-start(bf16[6,32,384]{2,1,0:T(8,128)(2,1)} %param.7), channel_id=1, source_target_pairs={{0,1},{1,2},{2,3},{3,4},{4,5},{5,6},{6,7},{7,0},{8,9},{9,10},{10,1... | collective-permute-start | bytes 442376 | tf_op jit(solution)/shard_map/ppermute | solution.py:28
  2.5 28.1 %collective-permute-start.1 = (bf16[6,32,384]{2,1,0:T(8,128)(2,1)}, bf16[6,32,384]{2,1,0:T(8,128)(2,1)S(1)}, u32[]{:S(2)}, u32[]{:S(2)}) collective-permute-start(bf16[6,32,384]{2,1,0:T(8,128)(2,1)} %param.7), channel_id=1, source_target_pairs={{0,7},{1,0},{2,1},{3,2},{4,3},{5,4},{6,5},{7,6},{8,15},{9,8},{10,9... | collective-permute-start | bytes 442376 | tf_op jit(solution)/shard_map/ppermute | solution.py:32
  6.4 5.6 %collective-permute-start.7 = (bf16[6,32,384]{2,1,0:T(8,128)(2,1)}, bf16[6,32,384]{2,1,0:T(8,128)(2,1)S(1)}, u32[]{:S(2)}, u32[]{:S(2)}) collective-permute-start(bf16[6,32,384]{2,1,0:T(8,128)(2,1)} %param.7), channel_id=1, source_target_pairs={{0,0},{4,1},{8,2},{12,3},{16,4},{20,5},{24,6},{28,7},{1,8},{5,9},{... | collective-permute-start | bytes 442376 | tf_op jit(solution)/shard_map/ppermute | solution.py:41
  12.0 34.1 %collective-permute-start.10 = (bf16[6,32,384]{2,1,0:T(8,128)(2,1)S(1)}, bf16[6,32,384]{2,1,0:T(8,128)(2,1)S(1)}, u32[]{:S(2)}, u32[]{:S(2)}) collective-permute-start(bf16[6,32,384]{2,1,0:T(8,128)(2,1)S(1)} %collective-permute-done.7.r0), channel_id=1, source_target_pairs={{0,24},{8,0},{16,8},{24,16},{1,25},{9,1},{17,9},{25,17},{2,26},{10... | collective-permute-start | bytes 442376 | tf_op jit(solution)/shard_map/ppermute | solution.py:42
  26.3 19.9 %collective-permute-start.8 = (bf16[6,32,384]{2,1,0:T(8,128)(2,1)S(1)}, bf16[6,32,384]{2,1,0:T(8,128)(2,1)S(1)}, u32[]{:S(2)}, u32[]{:S(2)}) collective-permute-start(bf16[6,32,384]{2,1,0:T(8,128)(2,1)S(1)} %collective-permute-done.7.r0), channel_id=1, source_target_pairs={{0,8},{8,16},{16,24},{24,0},{1,9},{9,17},{17,25},{25,1},{2,10},{10... | collective-permute-start | bytes 442376 | tf_op jit(solution)/shard_map/ppermute | solution.py:42
  26.3 19.9 %collective-permute-start.9 = (bf16[6,32,384]{2,1,0:T(8,128)(2,1)S(1)}, bf16[6,32,384]{2,1,0:T(8,128)(2,1)S(1)}, u32[]{:S(2)}, u32[]{:S(2)}) collective-permute-start(bf16[6,32,384]{2,1,0:T(8,128)(2,1)S(1)} %collective-permute-done.7.r0), channel_id=1, source_target_pairs={{0,16},{8,24},{16,0},{24,8},{1,17},{9,25},{17,1},{25,9},{2,18},{10... | collective-permute-start | bytes 442376 | tf_op jit(solution)/shard_map/ppermute | solution.py:42
  30.5 5.2 %collective-permute-start.2 = (bf16[6,32,384]{2,1,0:T(8,128)(2,1)S(1)}, bf16[6,32,384]{2,1,0:T(8,128)(2,1)S(1)}, u32[]{:S(2)}, u32[]{:S(2)}) collective-permute-start(bf16[6,32,384]{2,1,0:T(8,128)(2,1)S(1)} %collective-permute-done), channel_id=1, source_target_pairs={{0,1},{1,2},{2,3},{3,4},{4,5},{5,6},{6,7},{7,0},{8,9},{9,10},{10,1... | collective-permute-start | bytes 442376 | tf_op jit(solution)/shard_map/ppermute | solution.py:28
  30.5 5.2 %collective-permute-start.3 = (bf16[6,32,384]{2,1,0:T(8,128)(2,1)S(1)}, bf16[6,32,384]{2,1,0:T(8,128)(2,1)S(1)}, u32[]{:S(2)}, u32[]{:S(2)}) collective-permute-start(bf16[6,32,384]{2,1,0:T(8,128)(2,1)S(1)} %collective-permute-done.1), channel_id=1, source_target_pairs={{0,7},{1,0},{2,1},{3,2},{4,3},{5,4},{6,5},{7,6},{8,15},{9,8},{10,9... | collective-permute-start | bytes 442376 | tf_op jit(solution)/shard_map/ppermute | solution.py:32
  35.7 5.2 %collective-permute-start.4 = (bf16[6,32,384]{2,1,0:T(8,128)(2,1)S(1)}, bf16[6,32,384]{2,1,0:T(8,128)(2,1)S(1)}, u32[]{:S(2)}, u32[]{:S(2)}) collective-permute-start(bf16[6,32,384]{2,1,0:T(8,128)(2,1)S(1)} %collective-permute-done.2), channel_id=1, source_target_pairs={{0,1},{1,2},{2,3},{3,4},{4,5},{5,6},{6,7},{7,0},{8,9},{9,10},{10,1... | collective-permute-start | bytes 442376 | tf_op jit(solution)/shard_map/ppermute | solution.py:28
  35.7 5.2 %collective-permute-start.5 = (bf16[6,32,384]{2,1,0:T(8,128)(2,1)S(1)}, bf16[6,32,384]{2,1,0:T(8,128)(2,1)S(1)}, u32[]{:S(2)}, u32[]{:S(2)}) collective-permute-start(bf16[6,32,384]{2,1,0:T(8,128)(2,1)S(1)} %collective-permute-done.3), channel_id=1, source_target_pairs={{0,7},{1,0},{2,1},{3,2},{4,3},{5,4},{6,5},{7,6},{8,15},{9,8},{10,9... | collective-permute-start | bytes 442376 | tf_op jit(solution)/shard_map/ppermute | solution.py:32
  40.9 5.2 %collective-permute-start.6 = (bf16[6,32,384]{2,1,0:T(8,128)(2,1)S(1)}, bf16[6,32,384]{2,1,0:T(8,128)(2,1)S(1)}, u32[]{:S(2)}, u32[]{:S(2)}) collective-permute-start(bf16[6,32,384]{2,1,0:T(8,128)(2,1)S(1)} %collective-permute-done.4), channel_id=1, source_target_pairs={{0,1},{1,2},{2,3},{3,4},{4,5},{5,6},{6,7},{7,0},{8,9},{9,10},{10,1... | collective-permute-start | bytes 442376 | tf_op jit(solution)/shard_map/ppermute | solution.py:28
  46.1 56.0 %copy-start = (s32[6]{0:T(128)S(1)}, s32[6]{0:T(128)}, u32[]{:S(2)}) copy-start(s32[6]{0:T(128)} %param.10) | copy-start | bytes 76
  95.6 15.3 %all-to-all-start = ((f32[32,1,192]{2,1,0:T(1,128)}), f32[32,1,192]{2,1,0:T(1,128)S(1)}, u32[]{:S(2)}, u32[]{:S(2)}) async-start(f32[32,1,192]{2,1,0:T(1,128)} %all_to_all.13), calls=%async_computation | async-start | bytes 65536 | tf_op jit(solution)/shard_map/all_to_all | solution.py:104
  111.6 15.3 %all-to-all-start.1 = ((f32[8,1,192]{2,1,0:T(1,128)}), f32[8,1,192]{2,1,0:T(1,128)S(1)}, u32[]{:S(2)}, u32[]{:S(2)}) async-start(f32[8,1,192]{2,1,0:T(1,128)} %broadcast_in_dim.28), calls=%async_computation.1 | async-start | bytes 16384 | tf_op jit(solution)/shard_map/all_to_all | solution.py:106

commit v2 on v1

v2 whole, which is shorter than its diff:
```python
import functools

import jax
import jax.numpy as jnp
from jax import lax
from jax.experimental import pallas as pl
from jax.experimental.pallas import tpu as pltpu
from jax.sharding import PartitionSpec as P

F32 = jnp.float32
BF16 = jnp.bfloat16
NN = (((1,), (0,)), ((), ()))
NT = (((1,), (1,)), ((), ()))
BLOCK = 8
TILE = 64
SPAN = 512
LIMIT = 14


def dot(a, b, dims):
    return lax.dot_general(a, b, dims, preferred_element_type=F32)


def shift(size, by):
    return [(i, (i + by) % size) for i in range(size)]


def column_chunks(own, rows, cols):
    pairs = [(rows * j + g, g * cols + j) for g in range(rows) for j in range(cols)]
    first = lax.ppermute(own, ("grow", "gcol"), pairs)
    return [first] + [lax.ppermute(first, "grow", shift(rows, d)) for d in range(1, rows)]


def block_table(widths, depth):
    pairs = widths.shape[0]
    group = widths // BLOCK
    count = BLOCK * group * (group + 1) // 2 + (widths - BLOCK * group) * (group + 1)
    earlier = jnp.arange(pairs)[:, None] > jnp.arange(pairs)[None, :]
    start = jnp.sum(jnp.where(earlier, count[None, :], 0), axis=1)
    at = lax.iota(jnp.int32, 512)
    pair = jnp.sum((at[:, None] >= start[None, 1:]).astype(jnp.int32), axis=1)
    inside = at - jnp.sum(jnp.where(pair[:, None] == jnp.arange(pairs)[None, :], start[None, :], 0), axis=1)
    level = (inside >= 8).astype(jnp.int32) + (inside >= 24) + (inside >= 48)
    rest = inside - 4 * level * (level + 1)
    step = rest // (level + 1)
    first = pair * depth + BLOCK * (rest - step * (level + 1))
    partner = pair * depth + BLOCK * level + step
    total = jnp.sum(count)
    return jnp.where(at < total, 256 * first + partner, 0), total


def stage_kernel(backs, opens, closes, place, table, core_ref, *refs):
    refs = list(refs)
    n_chunks = len(backs)
    chunk_refs = [refs.pop(0) for _ in backs]
    if closes:
        right_chunks = [refs.pop(0) for _ in range(4)]
        amps_ref, live_ref = refs.pop(0), refs.pop(0)
    if not opens:
        refs.pop(0)
    m_ref = refs.pop(0)
    if closes:
        out_ref = refs.pop(0)
    core_v, panel, rho, sems = refs[:4]
    pairs, depth, chunk = chunk_refs[0].shape
    copies = []
    for u in range(n_chunks):
        rows = pl.ds(pl.multiple_of(lax.rem(place[2] + 8 - backs[u], 8) * chunk, chunk), chunk)
        copies.append(pltpu.make_async_copy(core_ref.at[rows], core_v.at[pl.ds(u * chunk, chunk)], sems.at[u]))
        copies[-1].start()
    for u in range(n_chunks):
        for p in range(pairs):
            panel[p * depth : (p + 1) * depth, u * chunk : (u + 1) * chunk] = chunk_refs[u][p].astype(F32)
    for copy in copies:
        copy.wait()
    total = place[0]

    def density(code):
        first = pl.multiple_of(lax.shift_right_logical(code, 8), BLOCK)
        return panel[pl.ds(first, BLOCK), :] * panel[pl.ds(lax.bitwise_and(code, 255), 1), :]

    def tile(start, blocks):
        def two(i, carry):
            both = [density(table[start + 2 * i]), density(table[start + 2 * i + 1])]
            rho[pl.ds(pl.multiple_of(16 * i, 16), 16), :] = jnp.concatenate(both, axis=0).astype(BF16)
            return carry

        lax.fori_loop(0, blocks // 2, two, 0, unroll=8)
        at = pl.ds(pl.multiple_of(start * BLOCK, 256), blocks * BLOCK)
        for s in range(0, core_v.shape[1], SPAN):
            term = dot(rho[: blocks * BLOCK, :], core_v[:, s : s + SPAN], NN)
            if opens:
                m_ref[at, s : s + SPAN] = term
            else:
                m_ref[at, s : s + SPAN] += term

    tiles = (total + TILE // 2 - 1) // TILE

    def full(t, carry):
        tile(t * TILE, TILE)
        return carry

    lax.fori_loop(0, tiles, full, 0)

    @pl.when(total > tiles * TILE)
    def _():
        tile(tiles * TILE, TILE // 2)

    if closes:
        right, proj, acc = refs[4:]
        for d, ref in enumerate(right_chunks):
            at = pl.multiple_of(lax.rem(place[1] + 4 - d, 4) * chunk, 128)
            right[:, :, pl.ds(at, chunk)] = ref[...]
        for p in range(pairs):
            rows = slice(p * depth, (p + 1) * depth)
            proj[rows, :] = dot(amps_ref[p], right[p], NN).astype(BF16).astype(F32)
        acc[...] = jnp.zeros_like(acc)

        def spread(i, carry):
            code = table[i]
            first = pl.multiple_of(lax.shift_right_logical(code, 8), BLOCK)
            partner = lax.bitwise_and(code, 255)
            term = m_ref[pl.ds(pl.multiple_of(i * BLOCK, BLOCK), BLOCK), :]
            acc[pl.ds(first, BLOCK), :] += term * proj[pl.ds(partner, 1), :]

            @pl.when(partner >= first + BLOCK)
            def _():
                mirrored = jnp.sum(term * proj[pl.ds(first, BLOCK), :], axis=0, keepdims=True)
                acc[pl.ds(partner, 1), :] += mirrored

            return carry

        lax.fori_loop(0, total, spread, 0)
        for p in range(pairs):
            rows = slice(p * depth, (p + 1) * depth)
            out_ref[p] = dot(acc[rows, :].astype(BF16), right[p], NT) * live_ref[p]


def stage(place, table, core, chunks, backs, state, ending=None):
    pairs, depth, chunk = chunks[0].shape
    width = core.shape[1]
    opens, closes = state is None, ending is not None
    inner = chunk * len(chunks)
    vmem = pl.BlockSpec(memory_space=pltpu.VMEM)
    smem = pl.BlockSpec(memory_space=pltpu.SMEM)
    args = [place, table, core, *chunks]
    specs = [smem, smem, pl.BlockSpec(memory_space=pltpu.HBM)] + [vmem] * len(chunks)
    if closes:
        args += ending
        specs += [vmem] * len(ending)
    if not opens:
        args.append(state)
        specs.append(vmem)
    rows = pairs * 80 * BLOCK
    scratch = [
        pltpu.VMEM((inner, width), BF16),
        pltpu.VMEM((pairs * depth, inner), F32),
        pltpu.VMEM((TILE * BLOCK, inner), BF16),
        pltpu.SemaphoreType.DMA((len(chunks),)),
    ]
    if closes:
        scratch += [
            pltpu.VMEM((pairs, depth, width), BF16),
            pltpu.VMEM((pairs * depth, width), F32),
            pltpu.VMEM((pairs * depth, width), F32),
        ]
    out = [pltpu.VMEM((rows, width), F32)]
    if closes:
        out.append(jax.ShapeDtypeStruct((pairs, depth, depth), F32))
    return pl.pallas_call(
        functools.partial(stage_kernel, backs, opens, closes),
        out_shape=out,
        in_specs=specs,
        out_specs=[vmem] * len(out),
        scratch_shapes=scratch,
        input_output_aliases={} if opens else {len(args) - 1: 0},
        cost_estimate=pl.CostEstimate(flops=2 * 2048 * inner * width, bytes_accessed=2 * inner * width, transcendentals=0),
        compiler_params=pltpu.CompilerParams(vmem_limit_bytes=LIMIT << 20),
    )(*args)[-1]


def local(core_matrix, pair_panels, amplitudes, pair_widths, batch_plan):
    pairs, depth, chunk = pair_panels.shape
    rows, cols = lax.axis_size("grow"), lax.axis_size("gcol")
    live = lax.broadcasted_iota(jnp.int32, (pairs, depth), 1) < pair_widths[:, None]
    live = live[:, :, None] & live[:, None, :]
    masked = jnp.where(live, amplitudes, 0)
    table, total = block_table(pair_widths, depth)
    place = jnp.stack([total, lax.axis_index("grow"), lax.axis_index("gcol")])
    masked, live, table, place = lax.optimization_barrier((masked, live.astype(F32), table, place))
    core_matrix = pltpu.with_memory_space_constraint(core_matrix, pltpu.HBM)
    run = functools.partial(stage, place, table, core_matrix)

    right = left = pair_panels
    state = run([pair_panels], (0,), None)
    for step in (1, 2):
        right = lax.ppermute(right, "gcol", shift(cols, 1))
        left = lax.ppermute(left, "gcol", shift(cols, -1))
        state = run([right, left], (step, -step), state)
    right = lax.ppermute(right, "gcol", shift(cols, 1))
    left = lax.ppermute(left, "gcol", shift(cols, -1))
    last = lax.ppermute(right, "gcol", shift(cols, 1))
    ending = [*column_chunks(pair_panels, rows, cols), masked, live]
    terms = run([right, left, last], (3, -3, 4), state, ending)
    parts = terms.reshape(pairs, rows * cols, depth * depth // (rows * cols))
    parts = parts.transpose(1, 0, 2).reshape(rows * cols, -1)
    mine = lax.all_to_all(parts, ("grow", "gcol"), 0, 0, tiled=True).sum(axis=0)
    copies = jnp.broadcast_to(mine, (lax.axis_size("pair"), *mine.shape))
    every = lax.all_to_all(copies, "pair", 0, 0, tiled=True)
    every = every.reshape(-1, depth * depth // (rows * cols))
    return every.at[batch_plan].get(mode="promise_in_bounds")


def solution(mesh):
    in_specs = (
        P("grow", "gcol"),
        P("pair", None, ("grow", "gcol")),
        P("pair", None, None),
        P("pair"),
        P("pair"),
    )
    out_specs = P("pair", ("grow", "gcol"))
    return jax.shard_map(local, mesh=mesh, in_specs=in_specs, out_specs=out_specs, check_vma=False)
```

time: 129 us -> 113 us (0.88)
  waiting for transfers between devices: 23 us -> 13.4 us
  Pallas kernels: 48.6 us -> 42.2 us
    ppermute x3, starting transfers between devices: 18.5 us -> 7.41 us  [column_chunks(): lax.ppermute(first, 'grow', shift(rows, d))]
    all_to_all x1, starting transfers between devices: 10.7 us -> 20.7 us  [local(): every = lax.all_to_all(copies, 'pair', 0, 0, tiled=True)]
    ppermute x7, waiting for transfers between devices: 9.61 us -> 0.02 us  [the longest x3 0.01 us: local(): right = lax.ppermute(right, 'gcol', shift(cols, 1))]
    pallas_call x1 -> x4, Pallas kernels: 48.6 us -> 42.2 us  [stage(): pl.pallas_call(functools.partial(stage_kernel, backs, opens, closes), out...]
    reduce_sum x0 -> x4, other arithmetic: none -> 1.66 us  [the longest x1 1.37 us: block_table(): total = jnp.sum(count)]
  transfers between devices with their start and end apart: 13 -> 13, of which waited for: 5 -> 2; matrix products, arithmetic and copies ran while one was open for 3% -> 4% of each run, Pallas kernels for 0% -> 21%
where the time goes in v2:
time: 113 us
  starting transfers between devices  48.9 us (43%)
  Pallas kernels  42.2 us (37%)
  waiting for transfers between devices  13.4 us (12%)
  other arithmetic  4.93 us (4%)
  local copies, waits for them, and re-layouts  3.59 us (3%)
    pallas_call x4, Pallas kernels, stage(): pl.pallas_call(functools.partial(stage_kernel, backs, opens, closes), out...  42.2 us
    all_to_all x1, starting transfers between devices, local(): every = lax.all_to_all(copies, 'pair', 0, 0, tiled=True)  20.7 us
    all_to_all x1, waiting for transfers between devices, local(): mine = lax.all_to_all(parts, ('grow', 'gcol'), 0, 0, tiled=True).sum(axis=0)  8.74 us
    ppermute x3, starting transfers between devices, column_chunks(): lax.ppermute(first, 'grow', shift(rows, d))  7.41 us
    ppermute x3, starting transfers between devices, local(): left = lax.ppermute(left, 'gcol', shift(cols, -1))  7.31 us
    all_to_all x1, starting transfers between devices, local(): mine = lax.all_to_all(parts, ('grow', 'gcol'), 0, 0, tiled=True).sum(axis=0)  6.13 us
    ppermute x3, starting transfers between devices, local(): right = lax.ppermute(right, 'gcol', shift(cols, 1))  5.75 us
    all_to_all x1, waiting for transfers between devices, local(): every = lax.all_to_all(copies, 'pair', 0, 0, tiled=True)  4.61 us
  transfers between devices with their start and end apart: 13, of which 2 were waited for; matrix products, arithmetic and copies ran while one was open for 4% of the time, Pallas kernels for 21%

profile of v2, /device:TPU:1, one launch (start us, length us, event | category | flops | bytes accessed | tf_op | source)
XLA Modules:
  0.0 113.1 jit_solution(8219288983738776352)
XLA Ops:
  0.0 2.5 %collective-permute-start = (bf16[6,32,384]{2,1,0:T(8,128)(2,1)}, bf16[6,32,384]{2,1,0:T(8,128)(2,1)S(1)}, u32[]{:S(2)}, u32[]{:S(2)}) collective-permute-start(bf16[6,32,384]{2,1,0:T(8,128)(2,1)} %refs_0_.1), channel_id=1, source_target_pairs={{0,1},{1,2},{2,3},{3,4},{4,5},{5,6},{6,7},{7,0},{8,9},{9,10},{10,1... | collective-permute-start | bytes 442376 | tf_op jit(solution)/shard_map/ppermute | solution.py:197
  2.5 3.9 %collective-permute-start.3 = (bf16[6,32,384]{2,1,0:T(8,128)(2,1)}, bf16[6,32,384]{2,1,0:T(8,128)(2,1)S(1)}, u32[]{:S(2)}, u32[]{:S(2)}) collective-permute-start(bf16[6,32,384]{2,1,0:T(8,128)(2,1)} %refs_0_.1), channel_id=1, source_target_pairs={{0,7},{1,0},{2,1},{3,2},{4,3},{5,4},{6,5},{7,6},{8,15},{9,8},{10,9... | collective-permute-start | bytes 442376 | tf_op jit(solution)/shard_map/ppermute | solution.py:198
  6.4 1.6 %collective-permute-start.7 = (bf16[6,32,384]{2,1,0:T(8,128)(2,1)}, bf16[6,32,384]{2,1,0:T(8,128)(2,1)S(1)}, u32[]{:S(2)}, u32[]{:S(2)}) collective-permute-start(bf16[6,32,384]{2,1,0:T(8,128)(2,1)} %refs_0_.1), channel_id=1, source_target_pairs={{0,0},{4,1},{8,2},{12,3},{16,4},{20,5},{24,6},{28,7},{1,8},{5,9},{... | collective-permute-start | bytes 442376 | tf_op jit(solution)/shard_map/ppermute | solution.py:30
  8.0 1.4 %fusion.1 = (s32[]{:T(128)}, s32[6]{0:T(128)S(1)}) fusion(s32[6]{0:T(128)} %param.8), kind=kLoop, calls=%fused_computation.32 | loop fusion | flops 221 | bytes 52 | tf_op jit(solution)/shard_map/reduce_sum | solution.py:48
  9.3 0.7 iota_compare_fusion.3
  10.1 0.1 select_reduce_fusion.1
  10.2 0.1 slice.3
  10.3 0.1 convert_reduce_fusion
  10.3 0.1 select_reduce_fusion
  10.4 0.1 and_convert_fusion.refs_8_
  10.5 0.9 and_select_fusion.refs_7_
  11.4 0.8 add_select_fusion.1.table
  12.2 0.7 pad_add_fusion.place
  12.9 0.0 collective-permute-done.refs_0_
  12.9 2.9 %collective-permute-start.1 = (bf16[6,32,384]{2,1,0:T(8,128)(2,1)S(1)}, bf16[6,32,384]{2,1,0:T(8,128)(2,1)S(1)}, u32[]{:S(2)}, u32[]{:S(2)}) collective-permute-start(bf16[6,32,384]{2,1,0:T(8,128)(2,1)S(1)} %collective-permute-done.refs_0_), channel_id=1, source_target_pairs={{0,1},{1,2},{2,3},{3,4},{4,5},{5,6},{6,7},{7,0},{8,9},{9,10},{10,1... | collective-permute-start | bytes 442376 | tf_op jit(solution)/shard_map/ppermute | solution.py:197
  15.8 0.9 copy-done
  16.7 6.4 %shard_map.55.refs_2_ = f32[3840,1536]{1,0:T(8,128)S(1)} custom-call(s32[3]{0:T(128)S(1)} %pad_add_fusion.place, s32[512]{0:T(512)S(1)} %add_select_fusion.1.table, bf16[3072,1536]{1,0:T(8,128)(2,1)} %core_ref.7, bf16[6,32,384]{2,1,0:T(8,128)(2,1)S(1)} %copy-done), custom_call_target="tpu_custom_call" | custom-call | flops 2415919104 | bytes 1179648 | tf_op jit(solution)/shard_map/pallas_call | solution.py:170
  23.1 0.0 collective-permute-done.7.refs_3_
  23.1 4.1 %collective-permute-start.10 = (bf16[6,32,384]{2,1,0:T(8,128)(2,1)S(1)}, bf16[6,32,384]{2,1,0:T(8,128)(2,1)S(1)}, u32[]{:S(2)}, u32[]{:S(2)}) collective-permute-start(bf16[6,32,384]{2,1,0:T(8,128)(2,1)S(1)} %collective-permute-done.7.refs_3_), channel_id=1, source_target_pairs={{0,24},{8,0},{16,8},{24,16},{1,25},{9,1},{17,9},{25,17},{2,26},{10... | collective-permute-start | bytes 442376 | tf_op jit(solution)/shard_map/ppermute | solution.py:31
  27.2 0.0 collective-permute-start.8
  27.2 3.3 %collective-permute-start.9 = (bf16[6,32,384]{2,1,0:T(8,128)(2,1)S(1)}, bf16[6,32,384]{2,1,0:T(8,128)(2,1)S(1)}, u32[]{:S(2)}, u32[]{:S(2)}) collective-permute-start(bf16[6,32,384]{2,1,0:T(8,128)(2,1)S(1)} %collective-permute-done.7.refs_3_), channel_id=1, source_target_pairs={{0,16},{8,24},{16,0},{24,8},{1,17},{9,25},{17,1},{25,9},{2,18},{10... | collective-permute-start | bytes 442376 | tf_op jit(solution)/shard_map/ppermute | solution.py:31
  30.5 0.0 collective-permute-done.3.refs_1_
  30.5 1.0 collective-permute-start.4
  31.5 0.0 collective-permute-done.1.refs_0_
  31.5 0.4 collective-permute-start.2
  32.0 8.4 %shard_map.56.refs_2_ = f32[3840,1536]{1,0:T(8,128)S(1)} custom-call(s32[3]{0:T(128)S(1)} %pad_add_fusion.place, s32[512]{0:T(512)S(1)} %add_select_fusion.1.table, bf16[3072,1536]{1,0:T(8,128)(2,1)} %core_ref.7, bf16[6,32,384]{2,1,0:T(8,128)(2,1)S(1)} %collective-permute-done.refs_0_, ...), custom_call_target="tpu_custom_call", output_to_operand_aliasing={{}: (5, {})} | custom-call | flops 4831838208 | bytes 2359296 | tf_op jit(solution)/shard_map/pallas_call | solution.py:170
  40.4 0.0 collective-permute-done.4.refs_1_
  40.4 2.3 %collective-permute-start.5 = (bf16[6,32,384]{2,1,0:T(8,128)(2,1)S(1)}, bf16[6,32,384]{2,1,0:T(8,128)(2,1)S(1)}, u32[]{:S(2)}, u32[]{:S(2)}) collective-permute-start(bf16[6,32,384]{2,1,0:T(8,128)(2,1)S(1)} %collective-permute-done.4.refs_1_), channel_id=1, source_target_pairs={{0,7},{1,0},{2,1},{3,2},{4,3},{5,4},{6,5},{7,6},{8,15},{9,8},{10,9... | collective-permute-start | bytes 442376 | tf_op jit(solution)/shard_map/ppermute | solution.py:201
  42.7 0.0 collective-permute-done.2.refs_0_
  42.7 0.0 collective-permute-start.6
  42.7 8.6 %shard_map.57.refs_9_ = f32[3840,1536]{1,0:T(8,128)S(1)} custom-call(s32[3]{0:T(128)S(1)} %pad_add_fusion.place, s32[512]{0:T(512)S(1)} %add_select_fusion.1.table, bf16[3072,1536]{1,0:T(8,128)(2,1)} %core_ref.7, bf16[6,32,384]{2,1,0:T(8,128)(2,1)S(1)} %collective-permute-done.1.refs_0_, ...), custom_call_target="tpu_custom_call", output_to_operand_aliasing={{}: (5, {})} | custom-call | flops 4831838208 | bytes 2359296 | tf_op jit(solution)/shard_map/pallas_call | solution.py:170
  51.3 0.0 copy-start.1
  51.3 0.0 collective-permute-done.10.refs_6_
  51.3 0.0 collective-permute-done.8.refs_4_
  51.3 0.0 collective-permute-done.9.refs_5_
  51.3 0.0 collective-permute-done.5.refs_1_
  51.4 0.0 collective-permute-done.6.refs_2_
  51.4 18.8 %shard_map.58 = (f32[3840,1536]{1,0:T(8,128)S(1)}, f32[6,32,32]{2,1,0:T(8,128)S(1)}) custom-call(s32[3]{0:T(128)S(1)} %pad_add_fusion.place, s32[512]{0:T(512)S(1)} %add_select_fusion.1.table, bf16[3072,1536]{1,0:T(8,128)(2,1)} %core_ref.7, bf16[6,32,384]{2,1,0:T(8,128)(2,1)S(1)} %collective-permute-done.2.refs_0_, ...), custom_call_target="tpu_custom_call", output_to_operand_aliasing={{0}: (12, {})} | custom-call | flops 7247757312 | bytes 3538944 | tf_op jit(solution)/shard_map/pallas_call | solution.py:170
  70.2 0.1 copy.12
  70.3 0.7 all_to_all.13
  71.0 6.1 %all-to-all-start = ((f32[32,1,192]{2,1,0:T(1,128)}), f32[32,1,192]{2,1,0:T(1,128)S(1)}, u32[]{:S(2)}, u32[]{:S(2)}) async-start(f32[32,1,192]{2,1,0:T(1,128)} %all_to_all.13), calls=%async_computation | async-start | bytes 65536 | tf_op jit(solution)/shard_map/all_to_all | solution.py:207
  77.1 8.7 %all-to-all-done = f32[32,1,192]{2,1,0:T(1,128)S(1)} async-done(((f32[32,1,192]{2,1,0:T(1,128)}), f32[32,1,192]{2,1,0:T(1,128)S(1)}, u32[]{:S(2)}, u32[]{:S(2)}) %all-to-all-start) | async-done | bytes 24608 | tf_op jit(solution)/shard_map/all_to_all | solution.py:207
  85.9 0.1 reduce_sum.49
  85.9 0.6 broadcast_in_dim.52
  86.5 20.7 %all-to-all-start.1 = ((f32[8,1,192]{2,1,0:T(1,128)}), f32[8,1,192]{2,1,0:T(1,128)S(1)}, u32[]{:S(2)}, u32[]{:S(2)}) async-start(f32[8,1,192]{2,1,0:T(1,128)} %broadcast_in_dim.52), calls=%async_computation.1 | async-start | bytes 16384 | tf_op jit(solution)/shard_map/all_to_all | solution.py:209
  107.3 4.6 %all-to-all-done.1 = f32[8,1,192]{2,1,0:T(1,128)S(1)} async-done(((f32[8,1,192]{2,1,0:T(1,128)}), f32[8,1,192]{2,1,0:T(1,128)S(1)}, u32[]{:S(2)}, u32[]{:S(2)}) %all-to-all-start.1) | async-done | bytes 6176 | tf_op jit(solution)/shard_map/all_to_all | solution.py:209
  111.9 0.1 reshape.48
  112.0 1.1 %gather_fusion = f32[6,32]{1,0:T(8,128)} fusion(f32[48,32]{1,0:T(8,128)S(1)} %reshape.48, s32[1024]{0:T(1024)S(1)} %pad_clamp_fusion), kind=kCustom, calls=%fused_computation | custom fusion | bytes 1560 | tf_op jit(solution)/shard_map/gather | solution.py:211
  (5 shorter events, 0.0 us)
Async XLA Ops:
  0.0 12.9 %collective-permute-start = (bf16[6,32,384]{2,1,0:T(8,128)(2,1)}, bf16[6,32,384]{2,1,0:T(8,128)(2,1)S(1)}, u32[]{:S(2)}, u32[]{:S(2)}) collective-permute-start(bf16[6,32,384]{2,1,0:T(8,128)(2,1)} %refs_0_.1), channel_id=1, source_target_pairs={{0,1},{1,2},{2,3},{3,4},{4,5},{5,6},{6,7},{7,0},{8,9},{9,10},{10,1... | collective-permute-start | bytes 442376 | tf_op jit(solution)/shard_map/ppermute | solution.py:197
  2.5 28.0 %collective-permute-start.3 = (bf16[6,32,384]{2,1,0:T(8,128)(2,1)}, bf16[6,32,384]{2,1,0:T(8,128)(2,1)S(1)}, u32[]{:S(2)}, u32[]{:S(2)}) collective-permute-start(bf16[6,32,384]{2,1,0:T(8,128)(2,1)} %refs_0_.1), channel_id=1, source_target_pairs={{0,7},{1,0},{2,1},{3,2},{4,3},{5,4},{6,5},{7,6},{8,15},{9,8},{10,9... | collective-permute-start | bytes 442376 | tf_op jit(solution)/shard_map/ppermute | solution.py:198
  6.4 16.7 %collective-permute-start.7 = (bf16[6,32,384]{2,1,0:T(8,128)(2,1)}, bf16[6,32,384]{2,1,0:T(8,128)(2,1)S(1)}, u32[]{:S(2)}, u32[]{:S(2)}) collective-permute-start(bf16[6,32,384]{2,1,0:T(8,128)(2,1)} %refs_0_.1), channel_id=1, source_target_pairs={{0,0},{4,1},{8,2},{12,3},{16,4},{20,5},{24,6},{28,7},{1,8},{5,9},{... | collective-permute-start | bytes 442376 | tf_op jit(solution)/shard_map/ppermute | solution.py:30
  12.9 18.6 %collective-permute-start.1 = (bf16[6,32,384]{2,1,0:T(8,128)(2,1)S(1)}, bf16[6,32,384]{2,1,0:T(8,128)(2,1)S(1)}, u32[]{:S(2)}, u32[]{:S(2)}) collective-permute-start(bf16[6,32,384]{2,1,0:T(8,128)(2,1)S(1)} %collective-permute-done.refs_0_), channel_id=1, source_target_pairs={{0,1},{1,2},{2,3},{3,4},{4,5},{5,6},{6,7},{7,0},{8,9},{9,10},{10,1... | collective-permute-start | bytes 442376 | tf_op jit(solution)/shard_map/ppermute | solution.py:197
  15.8 0.9 copy-start
  23.1 28.2 %collective-permute-start.10 = (bf16[6,32,384]{2,1,0:T(8,128)(2,1)S(1)}, bf16[6,32,384]{2,1,0:T(8,128)(2,1)S(1)}, u32[]{:S(2)}, u32[]{:S(2)}) collective-permute-start(bf16[6,32,384]{2,1,0:T(8,128)(2,1)S(1)} %collective-permute-done.7.refs_3_), channel_id=1, source_target_pairs={{0,24},{8,0},{16,8},{24,16},{1,25},{9,1},{17,9},{25,17},{2,26},{10... | collective-permute-start | bytes 442376 | tf_op jit(solution)/shard_map/ppermute | solution.py:31
  27.2 24.1 %collective-permute-start.8 = (bf16[6,32,384]{2,1,0:T(8,128)(2,1)S(1)}, bf16[6,32,384]{2,1,0:T(8,128)(2,1)S(1)}, u32[]{:S(2)}, u32[]{:S(2)}) collective-permute-start(bf16[6,32,384]{2,1,0:T(8,128)(2,1)S(1)} %collective-permute-done.7.refs_3_), channel_id=1, source_target_pairs={{0,8},{8,16},{16,24},{24,0},{1,9},{9,17},{17,25},{25,1},{2,10},{10... | collective-permute-start | bytes 442376 | tf_op jit(solution)/shard_map/ppermute | solution.py:31
  27.2 24.2 %collective-permute-start.9 = (bf16[6,32,384]{2,1,0:T(8,128)(2,1)S(1)}, bf16[6,32,384]{2,1,0:T(8,128)(2,1)S(1)}, u32[]{:S(2)}, u32[]{:S(2)}) collective-permute-start(bf16[6,32,384]{2,1,0:T(8,128)(2,1)S(1)} %collective-permute-done.7.refs_3_), channel_id=1, source_target_pairs={{0,16},{8,24},{16,0},{24,8},{1,17},{9,25},{17,1},{25,9},{2,18},{10... | collective-permute-start | bytes 442376 | tf_op jit(solution)/shard_map/ppermute | solution.py:31
  30.5 9.9 %collective-permute-start.4 = (bf16[6,32,384]{2,1,0:T(8,128)(2,1)S(1)}, bf16[6,32,384]{2,1,0:T(8,128)(2,1)S(1)}, u32[]{:S(2)}, u32[]{:S(2)}) collective-permute-start(bf16[6,32,384]{2,1,0:T(8,128)(2,1)S(1)} %collective-permute-done.3.refs_1_), channel_id=1, source_target_pairs={{0,7},{1,0},{2,1},{3,2},{4,3},{5,4},{6,5},{7,6},{8,15},{9,8},{10,9... | collective-permute-start | bytes 442376 | tf_op jit(solution)/shard_map/ppermute | solution.py:198
  31.5 11.2 %collective-permute-start.2 = (bf16[6,32,384]{2,1,0:T(8,128)(2,1)S(1)}, bf16[6,32,384]{2,1,0:T(8,128)(2,1)S(1)}, u32[]{:S(2)}, u32[]{:S(2)}) collective-permute-start(bf16[6,32,384]{2,1,0:T(8,128)(2,1)S(1)} %collective-permute-done.1.refs_0_), channel_id=1, source_target_pairs={{0,1},{1,2},{2,3},{3,4},{4,5},{5,6},{6,7},{7,0},{8,9},{9,10},{10,1... | collective-permute-start | bytes 442376 | tf_op jit(solution)/shard_map/ppermute | solution.py:200
  40.4 11.0 %collective-permute-start.5 = (bf16[6,32,384]{2,1,0:T(8,128)(2,1)S(1)}, bf16[6,32,384]{2,1,0:T(8,128)(2,1)S(1)}, u32[]{:S(2)}, u32[]{:S(2)}) collective-permute-start(bf16[6,32,384]{2,1,0:T(8,128)(2,1)S(1)} %collective-permute-done.4.refs_1_), channel_id=1, source_target_pairs={{0,7},{1,0},{2,1},{3,2},{4,3},{5,4},{6,5},{7,6},{8,15},{9,8},{10,9... | collective-permute-start | bytes 442376 | tf_op jit(solution)/shard_map/ppermute | solution.py:201
  42.7 8.6 %collective-permute-start.6 = (bf16[6,32,384]{2,1,0:T(8,128)(2,1)S(1)}, bf16[6,32,384]{2,1,0:T(8,128)(2,1)S(1)}, u32[]{:S(2)}, u32[]{:S(2)}) collective-permute-start(bf16[6,32,384]{2,1,0:T(8,128)(2,1)S(1)} %collective-permute-done.2.refs_0_), channel_id=1, source_target_pairs={{0,1},{1,2},{2,3},{3,4},{4,5},{5,6},{6,7},{7,0},{8,9},{9,10},{10,1... | collective-permute-start | bytes 442376 | tf_op jit(solution)/shard_map/ppermute | solution.py:202
  51.3 25.8 %copy-start.1 = (s32[6]{0:T(128)S(1)}, s32[6]{0:T(128)}, u32[]{:S(2)}) copy-start(s32[6]{0:T(128)} %param.9) | copy-start | bytes 76
  71.0 14.9 %all-to-all-start = ((f32[32,1,192]{2,1,0:T(1,128)}), f32[32,1,192]{2,1,0:T(1,128)S(1)}, u32[]{:S(2)}, u32[]{:S(2)}) async-start(f32[32,1,192]{2,1,0:T(1,128)} %all_to_all.13), calls=%async_computation | async-start | bytes 65536 | tf_op jit(solution)/shard_map/all_to_all | solution.py:207
  86.5 25.3 %all-to-all-start.1 = ((f32[8,1,192]{2,1,0:T(1,128)}), f32[8,1,192]{2,1,0:T(1,128)S(1)}, u32[]{:S(2)}, u32[]{:S(2)}) async-start(f32[8,1,192]{2,1,0:T(1,128)} %broadcast_in_dim.52), calls=%async_computation.1 | async-start | bytes 16384 | tf_op jit(solution)/shard_map/all_to_all | solution.py:209

commit v3 on v2

v3 whole, which is shorter than its diff:
```python
import functools

import jax
import jax.numpy as jnp
from jax import lax
from jax.experimental import pallas as pl
from jax.experimental.pallas import tpu as pltpu
from jax.sharding import PartitionSpec as P

F32 = jnp.float32
BF16 = jnp.bfloat16
NN = (((1,), (0,)), ((), ()))
NT = (((1,), (1,)), ((), ()))
BLOCK = 8
TILE = 64
LIMIT = 24


def dot(a, b, dims):
    return lax.dot_general(a, b, dims, preferred_element_type=F32)


def shift(size, by):
    return [(i, (i + by) % size) for i in range(size)]


def column_chunks(own, rows, cols):
    pairs = [(rows * j + g, g * cols + j) for g in range(rows) for j in range(cols)]
    first = lax.ppermute(own, ("grow", "gcol"), pairs)
    return [first] + [lax.ppermute(first, "grow", shift(rows, d)) for d in range(1, rows)]


def fill_table(widths, table, depth):
    at = jnp.int32(0)
    for p in range(widths.shape[0]):

        def partner(c, at):
            level = lax.shift_right_logical(c, 3)
            for i in range(depth // BLOCK):
                table[at + i] = 256 * (p * depth + BLOCK * i) + p * depth + c
            return at + level + 1

        at = lax.fori_loop(0, widths[p], partner, at)

    def clear(i, carry):
        table[at + i] = 0
        return carry

    lax.fori_loop(0, 2 * TILE, clear, 0, unroll=8)
    table[table.shape[0] - 1] = at


def row_targets(widths, total, start, rows, depth):
    at = start * BLOCK + lax.broadcasted_iota(jnp.int32, (1, rows), 1)
    block, offset = lax.shift_right_logical(at, 3), lax.bitwise_and(at, BLOCK - 1)
    begin = jnp.int32(0)
    base, inside = jnp.zeros_like(at), block
    for p in range(widths.shape[0] - 1):
        group = lax.shift_right_logical(widths[p], 3)
        begin = begin + 4 * group * (group + 1) + (widths[p] - BLOCK * group) * (group + 1)
        base = jnp.where(block >= begin, (p + 1) * depth, base)
        inside = jnp.where(block >= begin, block - begin, inside)
    level = jnp.where(inside >= 8, 1, 0) + jnp.where(inside >= 24, 1, 0) + jnp.where(inside >= 48, 1, 0)
    rest = inside - 4 * level * (level + 1)
    scale = jnp.where(level == 0, 256, jnp.where(level == 1, 128, jnp.where(level == 2, 86, 64)))
    step = lax.shift_right_logical(rest * scale, 8)
    first = BLOCK * (rest - step * (level + 1))
    here = block < total
    return (
        jnp.where(here, base + first + offset, -1),
        jnp.where(here & (first < BLOCK * level), base + BLOCK * level + step, -1),
    )


def stage_kernel(backs, opens, closes, *refs):
    refs = list(refs)
    widths, core_ref = refs.pop(0), refs.pop(0)
    chunk_refs = [refs.pop(0) for _ in backs]
    if closes:
        right_chunks = [refs.pop(0) for _ in range(4)]
        amps_ref = refs.pop(0)
    if not opens:
        table = refs.pop(0)
        refs.pop(0)
    m_ref = refs.pop(0)
    if opens:
        table = refs.pop(0)
    if closes:
        out_ref = refs.pop(0)
    core_v, panel, rho_a, rho_b, sems = refs[:5]
    pairs, depth, chunk = chunk_refs[0].shape
    me = lax.axis_index("gcol")
    copies = []
    if opens:
        own = refs[5]
        copies.append(pltpu.make_async_copy(chunk_refs[0], own, sems.at[len(backs)]))
        copies[-1].start()
        chunk_refs = [own]
    for u, back in enumerate(backs):
        rows = pl.ds(pl.multiple_of(lax.rem(me + 8 - back, 8) * chunk, chunk), chunk)
        copies.append(pltpu.make_async_copy(core_ref.at[rows], core_v.at[pl.ds(u * chunk, chunk)], sems.at[u]))
        copies[-1].start()
    if opens:
        fill_table(widths, table, depth)
        copies.pop(0).wait()
    for u in range(len(backs)):
        for p in range(pairs):
            panel[p * depth : (p + 1) * depth, u * chunk : (u + 1) * chunk] = chunk_refs[u][p].astype(F32)
    total = table[table.shape[0] - 1]

    def density(code):
        first = pl.multiple_of(lax.shift_right_logical(code, 8), BLOCK)
        return panel[pl.ds(first, BLOCK), :] * panel[pl.ds(lax.bitwise_and(code, 255), 1), :]

    def build(rho, start):
        for i in range(TILE // 2):
            both = [density(table[start + 2 * i]), density(table[start + 2 * i + 1])]
            rho[16 * i : 16 * (i + 1), :] = jnp.concatenate(both, axis=0).astype(BF16)

    if closes:
        right, proj, term_a, term_b, acc = refs[5:]
        for d, ref in enumerate(right_chunks):
            at = pl.multiple_of(lax.rem(lax.axis_index("grow") + 4 - d, 4) * chunk, 128)
            for p in range(pairs):
                right[p * depth : (p + 1) * depth, pl.ds(at, chunk)] = ref[p]
        live = []
        for p in range(pairs):
            rows = slice(p * depth, (p + 1) * depth)
            spot = [lax.broadcasted_iota(jnp.int32, (depth, depth), k) < widths[p] for k in (0, 1)]
            live.append(spot[0] & spot[1])
            masked = jnp.where(live[p], amps_ref[p].astype(F32), 0.0).astype(BF16)
            proj[rows, :] = dot(masked, right[rows, :], NN).astype(BF16).astype(F32)
        acc[...] = jnp.zeros_like(acc)

    def finish(start, blocks):
        def two(i, carry):
            plain, mirrored = [], []
            for k in range(2):
                code = table[start + 2 * i + k]
                first = pl.multiple_of(lax.shift_right_logical(code, 8), BLOCK)
                at = pl.multiple_of((start + 2 * i + k) * BLOCK, BLOCK)
                term = m_ref[pl.ds(at, BLOCK), :]
                plain.append(term * proj[pl.ds(lax.bitwise_and(code, 255), 1), :])
                mirrored.append(term * proj[pl.ds(first, BLOCK), :])
            at = pl.ds(pl.multiple_of(16 * i, 16), 16)
            term_a[at, :] = jnp.concatenate(plain, axis=0).astype(BF16)
            term_b[at, :] = jnp.concatenate(mirrored, axis=0).astype(BF16)
            return carry

        lax.fori_loop(0, blocks // 2, two, 0, unroll=4)
        rows = blocks * BLOCK
        orbital = lax.broadcasted_iota(jnp.int32, (pairs * depth, rows), 0)
        for target, term in zip(row_targets(widths, total, start, rows, depth), (term_a, term_b)):
            pick = jnp.where(orbital == target, 1.0, 0.0).astype(BF16)
            acc[...] += dot(pick, dot(term[:rows, :], right[...], NT).astype(BF16), NN)

    def multiply(rho, start, blocks):
        at = pl.ds(pl.multiple_of(start * BLOCK, 256), blocks * BLOCK)
        term = dot(rho[: blocks * BLOCK, :], core_v[...], NN)
        if opens:
            m_ref[at, :] = term
        else:
            m_ref[at, :] += term
        if closes:
            finish(start, blocks)

    def step(rho, later, t):
        build(later, (t + 1) * TILE)
        multiply(rho, t * TILE, TILE)

    build(rho_a, 0)
    for copy in copies:
        copy.wait()
    tiles = (total + TILE // 2 - 1) // TILE

    def two_steps(i, carry):
        step(rho_a, rho_b, 2 * i)

        @pl.when(2 * i + 1 < tiles)
        def _():
            step(rho_b, rho_a, 2 * i + 1)

        return carry

    lax.fori_loop(0, (tiles + 1) // 2, two_steps, 0)
    odd = lax.rem(tiles, 2)
    for k, rho in enumerate((rho_a, rho_b)):

        @pl.when((total > tiles * TILE) & (odd == k))
        def _(rho=rho):
            multiply(rho, tiles * TILE, TILE // 2)

    if closes:
        for p in range(pairs):
            rows = slice(p * depth, (p + 1) * depth)
            out_ref[:, rows] = jnp.where(live[p], acc[rows, rows], 0.0)


def stage(widths, core, chunks, backs, state, ending=()):
    pairs, depth, chunk = chunks[0].shape
    width = core.shape[1]
    opens, closes = state is None, len(ending) > 0
    inner = chunk * len(chunks)
    vmem = pl.BlockSpec(memory_space=pltpu.VMEM)
    smem = pl.BlockSpec(memory_space=pltpu.SMEM)
    hbm = pl.BlockSpec(memory_space=pltpu.HBM)
    args = [widths, core, *chunks, *ending]
    specs = [smem, hbm] + [hbm if opens else vmem] * len(chunks) + [vmem] * len(ending)
    if not opens:
        args += [state[1], state[0]]
        specs += [smem, vmem]
    rows = pairs * depth
    most = pairs * BLOCK * sum(range(1, depth // BLOCK + 1))
    scratch = [
        pltpu.VMEM((inner, width), BF16),
        pltpu.VMEM((rows, inner), F32),
        pltpu.VMEM((TILE * BLOCK, inner), BF16),
        pltpu.VMEM((TILE * BLOCK, inner), BF16),
        pltpu.SemaphoreType.DMA((len(chunks) + 1,)),
    ]
    out, out_specs = [pltpu.VMEM((most * BLOCK, width), F32)], [vmem]
    if opens:
        scratch.append(pltpu.VMEM((pairs, depth, chunk), BF16))
        out.append(jax.ShapeDtypeStruct((most + 3 * TILE,), jnp.int32))
        out_specs.append(smem)
    if closes:
        scratch += [
            pltpu.VMEM((rows, width), BF16),
            pltpu.VMEM((rows, width), F32),
            pltpu.VMEM((TILE * BLOCK, width), BF16),
            pltpu.VMEM((TILE * BLOCK, width), BF16),
            pltpu.VMEM((rows, rows), F32),
        ]
        out.append(jax.ShapeDtypeStruct((depth, rows), F32))
        out_specs.append(vmem)
    results = pl.pallas_call(
        functools.partial(stage_kernel, backs, opens, closes),
        out_shape=out,
        in_specs=specs,
        out_specs=out_specs,
        scratch_shapes=scratch,
        input_output_aliases={} if opens else {len(args) - 1: 0},
        cost_estimate=pl.CostEstimate(flops=2 * 2048 * inner * width, bytes_accessed=2 * inner * width, transcendentals=0),
        compiler_params=pltpu.CompilerParams(vmem_limit_bytes=LIMIT << 20),
    )(*args)
    if closes:
        return results[1]
    return (results[0], results[1] if opens else state[1])


def local(core_matrix, pair_panels, amplitudes, pair_widths, batch_plan):
    rows, cols = lax.axis_size("grow"), lax.axis_size("gcol")
    core_matrix = pltpu.with_memory_space_constraint(core_matrix, pltpu.HBM)
    run = functools.partial(stage, pair_widths, core_matrix)

    right = left = pair_panels
    state = run([pltpu.with_memory_space_constraint(pair_panels, pltpu.HBM)], (0,), None)
    for step in (1, 2):
        right = lax.ppermute(right, "gcol", shift(cols, 1))
        left = lax.ppermute(left, "gcol", shift(cols, -1))
        state = run([right, left], (step, -step), state)
    right = lax.ppermute(right, "gcol", shift(cols, 1))
    left = lax.ppermute(left, "gcol", shift(cols, -1))
    last = lax.ppermute(right, "gcol", shift(cols, 1))
    ending = [*column_chunks(pair_panels, rows, cols), amplitudes]
    parts = run([right, left, last], (3, -3, 4), state, ending)
    mine = lax.all_to_all(parts, ("grow", "gcol"), 0, 0, tiled=True).sum(axis=0)
    copies = jnp.broadcast_to(mine, (lax.axis_size("pair"), *mine.shape))
    every = lax.all_to_all(copies, "pair", 0, 0, tiled=True)
    every = every.reshape(-1, parts.shape[0])
    return every.at[batch_plan].get(mode="promise_in_bounds")


def solution(mesh):
    in_specs = (
        P("grow", "gcol"),
        P("pair", None, ("grow", "gcol")),
        P("pair", None, None),
        P("pair"),
        P("pair"),
    )
    out_specs = P("pair", ("grow", "gcol"))
    return jax.shard_map(local, mesh=mesh, in_specs=in_specs, out_specs=out_specs, check_vma=False)
```

time: 113 us -> 112 us (level); the launches traced: 113 us -> 114 us
  Pallas kernels: 42.2 us -> 56.5 us
  starting transfers between devices: 48.9 us -> 38.5 us
  other arithmetic: 4.93 us -> 0.09 us
  waiting for transfers between devices: 13.4 us -> 15.6 us
    pallas_call x4, Pallas kernels: 42.2 us -> 56.5 us  [stage(): pl.pallas_call(functools.partial(stage_kernel, backs, opens, closes), out...]
    all_to_all x1, starting transfers between devices: 20.7 us -> 8.68 us  [local(): every = lax.all_to_all(copies, 'pair', 0, 0, tiled=True)]
    ppermute x3, starting transfers between devices: 7.41 us -> 11.1 us  [column_chunks(): lax.ppermute(first, 'grow', shift(rows, d))]
    ppermute x3, waiting for transfers between devices: 0.01 us -> 2.23 us  [local(): right = lax.ppermute(right, 'gcol', shift(cols, 1))]
    ppermute x3, starting transfers between devices: 5.75 us -> 3.65 us  [local(): right = lax.ppermute(right, 'gcol', shift(cols, 1))]
    select_n x2 -> x0, other arithmetic: 1.66 us -> none  [the longest x1 0.89 us: local(): masked = jnp.where(live, amplitudes, 0)]
    reduce_sum x4 -> x0, other arithmetic: 1.66 us -> none  [the longest x1 1.37 us: block_table(): total = jnp.sum(count)]
  transfers between devices with their start and end apart: 13 -> 13, of which waited for: 2 -> 3; matrix products, arithmetic and copies ran while one was open for 4% -> 0% of each run, Pallas kernels for 21% -> 24%
where the time goes in v3:
time: 112 us; the launch traced here: 114 us
  Pallas kernels  56.5 us (50%)
  starting transfers between devices  38.5 us (34%)
  waiting for transfers between devices  15.6 us (14%)
  local copies, waits for them, and re-layouts  3.13 us (3%)
    pallas_call x4, Pallas kernels, stage(): pl.pallas_call(functools.partial(stage_kernel, backs, opens, closes), out...  56.5 us
    ppermute x3, starting transfers between devices, column_chunks(): lax.ppermute(first, 'grow', shift(rows, d))  11.1 us
    all_to_all x1, waiting for transfers between devices, local(): mine = lax.all_to_all(parts, ('grow', 'gcol'), 0, 0, tiled=True).sum(axis=0)  8.74 us
    all_to_all x1, starting transfers between devices, local(): every = lax.all_to_all(copies, 'pair', 0, 0, tiled=True)  8.68 us
    ppermute x3, starting transfers between devices, local(): left = lax.ppermute(left, 'gcol', shift(cols, -1))  7.36 us
    all_to_all x1, starting transfers between devices, local(): mine = lax.all_to_all(parts, ('grow', 'gcol'), 0, 0, tiled=True).sum(axis=0)  6.1 us
    all_to_all x1, waiting for transfers between devices, local(): every = lax.all_to_all(copies, 'pair', 0, 0, tiled=True)  4.61 us
    ppermute x3, starting transfers between devices, local(): right = lax.ppermute(right, 'gcol', shift(cols, 1))  3.65 us
  transfers between devices with their start and end apart: 13, of which 3 were waited for; matrix products, arithmetic and copies ran while one was open for 0% of the time, Pallas kernels for 24%

profile of v3, /device:TPU:1, one launch (start us, length us, event | category | flops | bytes accessed | tf_op | source)
XLA Modules:
  0.0 113.9 jit_solution(3575930628333547845)
XLA Ops:
  0.0 2.5 %collective-permute-start = (bf16[6,32,384]{2,1,0:T(8,128)(2,1)}, bf16[6,32,384]{2,1,0:T(8,128)(2,1)S(1)}, u32[]{:S(2)}, u32[]{:S(2)}) collective-permute-start(bf16[6,32,384]{2,1,0:T(8,128)(2,1)} %refs_2_.1), channel_id=1, source_target_pairs={{0,1},{1,2},{2,3},{3,4},{4,5},{5,6},{6,7},{7,0},{8,9},{9,10},{10,1... | collective-permute-start | bytes 442376 | tf_op jit(solution)/shard_map/ppermute | solution.py:259
  2.5 3.9 %collective-permute-start.3 = (bf16[6,32,384]{2,1,0:T(8,128)(2,1)}, bf16[6,32,384]{2,1,0:T(8,128)(2,1)S(1)}, u32[]{:S(2)}, u32[]{:S(2)}) collective-permute-start(bf16[6,32,384]{2,1,0:T(8,128)(2,1)} %refs_2_.1), channel_id=1, source_target_pairs={{0,7},{1,0},{2,1},{3,2},{4,3},{5,4},{6,5},{7,6},{8,15},{9,8},{10,9... | collective-permute-start | bytes 442376 | tf_op jit(solution)/shard_map/ppermute | solution.py:260
  6.4 1.6 %collective-permute-start.7 = (bf16[6,32,384]{2,1,0:T(8,128)(2,1)}, bf16[6,32,384]{2,1,0:T(8,128)(2,1)S(1)}, u32[]{:S(2)}, u32[]{:S(2)}) collective-permute-start(bf16[6,32,384]{2,1,0:T(8,128)(2,1)} %refs_2_.1), channel_id=1, source_target_pairs={{0,0},{4,1},{8,2},{12,3},{16,4},{20,5},{24,6},{28,7},{1,8},{5,9},{... | collective-permute-start | bytes 442376 | tf_op jit(solution)/shard_map/ppermute | solution.py:29
  8.0 2.2 %collective-permute-done.refs_2_ = bf16[6,32,384]{2,1,0:T(8,128)(2,1)S(1)} collective-permute-done((bf16[6,32,384]{2,1,0:T(8,128)(2,1)}, bf16[6,32,384]{2,1,0:T(8,128)(2,1)S(1)}, u32[]{:S(2)}, u32[]{:S(2)}) %collective-permute-start) | collective-permute-done | bytes 147488 | tf_op jit(solution)/shard_map/ppermute | solution.py:259
  10.2 0.7 collective-permute-start.1
  10.9 0.0 copy-start.1
  10.9 0.7 copy-done.1
  11.5 7.8 %shard_map.55 = (f32[3840,1536]{1,0:T(8,128)S(1)}, s32[672]{0:T(1024)S(1)}) custom-call(s32[6]{0:T(128)S(1)} %copy-done.1, bf16[3072,1536]{1,0:T(8,128)(2,1)} %refs_1_.7, bf16[6,32,384]{2,1,0:T(8,128)(2,1)} %refs_2_.1), custom_call_target="tpu_custom_call" | custom-call | flops 2415919104 | bytes 1179648 | tf_op jit(solution)/shard_map/pallas_call | solution.py:236
  19.4 0.0 collective-permute-done.7.refs_5_
  19.4 6.9 %collective-permute-start.10 = (bf16[6,32,384]{2,1,0:T(8,128)(2,1)S(1)}, bf16[6,32,384]{2,1,0:T(8,128)(2,1)S(1)}, u32[]{:S(2)}, u32[]{:S(2)}) collective-permute-start(bf16[6,32,384]{2,1,0:T(8,128)(2,1)S(1)} %collective-permute-done.7.refs_5_), channel_id=1, source_target_pairs={{0,24},{8,0},{16,8},{24,16},{1,25},{9,1},{17,9},{25,17},{2,26},{10... | collective-permute-start | bytes 442376 | tf_op jit(solution)/shard_map/ppermute | solution.py:30
  26.3 0.0 collective-permute-start.8
  26.3 4.2 %collective-permute-start.9 = (bf16[6,32,384]{2,1,0:T(8,128)(2,1)S(1)}, bf16[6,32,384]{2,1,0:T(8,128)(2,1)S(1)}, u32[]{:S(2)}, u32[]{:S(2)}) collective-permute-start(bf16[6,32,384]{2,1,0:T(8,128)(2,1)S(1)} %collective-permute-done.7.refs_5_), channel_id=1, source_target_pairs={{0,16},{8,24},{16,0},{24,8},{1,17},{9,25},{17,1},{25,9},{2,18},{10... | collective-permute-start | bytes 442376 | tf_op jit(solution)/shard_map/ppermute | solution.py:30
  30.5 0.0 collective-permute-done.3.refs_3_
  30.5 1.0 collective-permute-start.4
  31.5 0.0 collective-permute-done.1.refs_2_
  31.5 0.5 collective-permute-start.2
  32.0 9.6 %shard_map.56.refs_5_ = f32[3840,1536]{1,0:T(8,128)S(1)} custom-call(s32[6]{0:T(128)S(1)} %copy-done.1, bf16[3072,1536]{1,0:T(8,128)(2,1)} %refs_1_.7, bf16[6,32,384]{2,1,0:T(8,128)(2,1)S(1)} %collective-permute-done.refs_2_, bf16[6,32,384]{2,1,0:T(8,128)(2,1)S(1)} %collective-permute-done.3.refs_3_, ...), custom_call_target="tpu_custom_call", output_to_operand_aliasing={{}: (5, {})} | custom-call | flops 4831838208 | bytes 2359296 | tf_op jit(solution)/shard_map/pallas_call | solution.py:236
  41.6 0.0 copy-start
  41.6 0.0 collective-permute-done.4.refs_3_
  41.6 2.4 %collective-permute-start.5 = (bf16[6,32,384]{2,1,0:T(8,128)(2,1)S(1)}, bf16[6,32,384]{2,1,0:T(8,128)(2,1)S(1)}, u32[]{:S(2)}, u32[]{:S(2)}) collective-permute-start(bf16[6,32,384]{2,1,0:T(8,128)(2,1)S(1)} %collective-permute-done.4.refs_3_), channel_id=1, source_target_pairs={{0,7},{1,0},{2,1},{3,2},{4,3},{5,4},{6,5},{7,6},{8,15},{9,8},{10,9... | collective-permute-start | bytes 442376 | tf_op jit(solution)/shard_map/ppermute | solution.py:263
  44.0 0.0 collective-permute-done.2.refs_2_
  44.0 0.0 collective-permute-start.6
  44.0 9.6 %shard_map.57.refs_11_ = f32[3840,1536]{1,0:T(8,128)S(1)} custom-call(s32[6]{0:T(128)S(1)} %copy-done.1, bf16[3072,1536]{1,0:T(8,128)(2,1)} %refs_1_.7, bf16[6,32,384]{2,1,0:T(8,128)(2,1)S(1)} %collective-permute-done.1.refs_2_, bf16[6,32,384]{2,1,0:T(8,128)(2,1)S(1)} %collective-permute-done.4.refs_3_, ...), custom_call_target="tpu_custom_call", output_to_operand_aliasing={{}: (5, {})} | custom-call | flops 4831838208 | bytes 2359296 | tf_op jit(solution)/shard_map/pallas_call | solution.py:236
  53.7 0.0 copy-start.2
  53.7 0.0 collective-permute-done.10.refs_8_
  53.7 0.0 collective-permute-done.8.refs_6_
  53.7 0.0 collective-permute-done.9.refs_7_
  53.7 0.0 collective-permute-done.5.refs_3_
  53.7 0.0 collective-permute-done.6.refs_4_
  53.7 0.0 copy-done
  53.7 29.4 %shard_map.58 = (f32[3840,1536]{1,0:T(8,128)S(1)}, f32[32,192]{1,0:T(8,128)S(1)}) custom-call(s32[6]{0:T(128)S(1)} %copy-done.1, bf16[3072,1536]{1,0:T(8,128)(2,1)} %refs_1_.7, bf16[6,32,384]{2,1,0:T(8,128)(2,1)S(1)} %collective-permute-done.2.refs_2_, bf16[6,32,384]{2,1,0:T(8,128)(2,1)S(1)} %collective-permute-done.5.refs_3_, ...), custom_call_target="tpu_custom_call", output_to_operand_aliasing={{0}: (11, {})} | custom-call | flops 7247757312 | bytes 3538944 | tf_op jit(solution)/shard_map/pallas_call | solution.py:236
  83.2 0.6 copy.9
  83.8 6.1 %all-to-all-start = ((f32[32,1,192]{2,1,0:T(1,128)}), f32[32,1,192]{2,1,0:T(1,128)S(1)}, u32[]{:S(2)}, u32[]{:S(2)}) async-start(f32[32,1,192]{2,1,0:T(1,128)} %copy.9), calls=%async_computation | async-start | bytes 65536 | tf_op jit(solution)/shard_map/all_to_all | solution.py:267
  89.9 0.0 copy-done.2
  89.9 8.7 %all-to-all-done = f32[32,1,192]{2,1,0:T(1,128)S(1)} async-done(((f32[32,1,192]{2,1,0:T(1,128)}), f32[32,1,192]{2,1,0:T(1,128)S(1)}, u32[]{:S(2)}, u32[]{:S(2)}) %all-to-all-start) | async-done | bytes 24608 | tf_op jit(solution)/shard_map/all_to_all | solution.py:267
  98.7 0.1 reduce_sum.9
  98.7 0.6 broadcast_in_dim.6
  99.3 8.7 %all-to-all-start.1 = ((f32[8,1,192]{2,1,0:T(1,128)}), f32[8,1,192]{2,1,0:T(1,128)S(1)}, u32[]{:S(2)}, u32[]{:S(2)}) async-start(f32[8,1,192]{2,1,0:T(1,128)} %broadcast_in_dim.6), calls=%async_computation.1 | async-start | bytes 16384 | tf_op jit(solution)/shard_map/all_to_all | solution.py:269
  108.0 4.6 %all-to-all-done.1 = f32[8,1,192]{2,1,0:T(1,128)S(1)} async-done(((f32[8,1,192]{2,1,0:T(1,128)}), f32[8,1,192]{2,1,0:T(1,128)S(1)}, u32[]{:S(2)}, u32[]{:S(2)}) %all-to-all-start.1) | async-done | bytes 6176 | tf_op jit(solution)/shard_map/all_to_all | solution.py:269
  112.7 0.1 reshape.10
  112.7 1.1 %gather_fusion = f32[6,32]{1,0:T(8,128)} fusion(f32[48,32]{1,0:T(8,128)S(1)} %reshape.10, s32[1024]{0:T(1024)S(1)} %pad_clamp_fusion), kind=kCustom, calls=%fused_computation | custom fusion | bytes 1560 | tf_op jit(solution)/shard_map/gather | solution.py:271
  (3 shorter events, 0.0 us)
Async XLA Ops:
  0.0 10.2 %collective-permute-start = (bf16[6,32,384]{2,1,0:T(8,128)(2,1)}, bf16[6,32,384]{2,1,0:T(8,128)(2,1)S(1)}, u32[]{:S(2)}, u32[]{:S(2)}) collective-permute-start(bf16[6,32,384]{2,1,0:T(8,128)(2,1)} %refs_2_.1), channel_id=1, source_target_pairs={{0,1},{1,2},{2,3},{3,4},{4,5},{5,6},{6,7},{7,0},{8,9},{9,10},{10,1... | collective-permute-start | bytes 442376 | tf_op jit(solution)/shard_map/ppermute | solution.py:259
  2.5 28.0 %collective-permute-start.3 = (bf16[6,32,384]{2,1,0:T(8,128)(2,1)}, bf16[6,32,384]{2,1,0:T(8,128)(2,1)S(1)}, u32[]{:S(2)}, u32[]{:S(2)}) collective-permute-start(bf16[6,32,384]{2,1,0:T(8,128)(2,1)} %refs_2_.1), channel_id=1, source_target_pairs={{0,7},{1,0},{2,1},{3,2},{4,3},{5,4},{6,5},{7,6},{8,15},{9,8},{10,9... | collective-permute-start | bytes 442376 | tf_op jit(solution)/shard_map/ppermute | solution.py:260
  6.4 13.0 %collective-permute-start.7 = (bf16[6,32,384]{2,1,0:T(8,128)(2,1)}, bf16[6,32,384]{2,1,0:T(8,128)(2,1)S(1)}, u32[]{:S(2)}, u32[]{:S(2)}) collective-permute-start(bf16[6,32,384]{2,1,0:T(8,128)(2,1)} %refs_2_.1), channel_id=1, source_target_pairs={{0,0},{4,1},{8,2},{12,3},{16,4},{20,5},{24,6},{28,7},{1,8},{5,9},{... | collective-permute-start | bytes 442376 | tf_op jit(solution)/shard_map/ppermute | solution.py:29
  10.2 21.3 %collective-permute-start.1 = (bf16[6,32,384]{2,1,0:T(8,128)(2,1)S(1)}, bf16[6,32,384]{2,1,0:T(8,128)(2,1)S(1)}, u32[]{:S(2)}, u32[]{:S(2)}) collective-permute-start(bf16[6,32,384]{2,1,0:T(8,128)(2,1)S(1)} %collective-permute-done.refs_2_), channel_id=1, source_target_pairs={{0,1},{1,2},{2,3},{3,4},{4,5},{5,6},{6,7},{7,0},{8,9},{9,10},{10,1... | collective-permute-start | bytes 442376 | tf_op jit(solution)/shard_map/ppermute | solution.py:259
  10.9 0.7 copy-start.1
  19.4 34.3 %collective-permute-start.10 = (bf16[6,32,384]{2,1,0:T(8,128)(2,1)S(1)}, bf16[6,32,384]{2,1,0:T(8,128)(2,1)S(1)}, u32[]{:S(2)}, u32[]{:S(2)}) collective-permute-start(bf16[6,32,384]{2,1,0:T(8,128)(2,1)S(1)} %collective-permute-done.7.refs_5_), channel_id=1, source_target_pairs={{0,24},{8,0},{16,8},{24,16},{1,25},{9,1},{17,9},{25,17},{2,26},{10... | collective-permute-start | bytes 442376 | tf_op jit(solution)/shard_map/ppermute | solution.py:30
  26.3 27.4 %collective-permute-start.8 = (bf16[6,32,384]{2,1,0:T(8,128)(2,1)S(1)}, bf16[6,32,384]{2,1,0:T(8,128)(2,1)S(1)}, u32[]{:S(2)}, u32[]{:S(2)}) collective-permute-start(bf16[6,32,384]{2,1,0:T(8,128)(2,1)S(1)} %collective-permute-done.7.refs_5_), channel_id=1, source_target_pairs={{0,8},{8,16},{16,24},{24,0},{1,9},{9,17},{17,25},{25,1},{2,10},{10... | collective-permute-start | bytes 442376 | tf_op jit(solution)/shard_map/ppermute | solution.py:30
  26.3 27.4 %collective-permute-start.9 = (bf16[6,32,384]{2,1,0:T(8,128)(2,1)S(1)}, bf16[6,32,384]{2,1,0:T(8,128)(2,1)S(1)}, u32[]{:S(2)}, u32[]{:S(2)}) collective-permute-start(bf16[6,32,384]{2,1,0:T(8,128)(2,1)S(1)} %collective-permute-done.7.refs_5_), channel_id=1, source_target_pairs={{0,16},{8,24},{16,0},{24,8},{1,17},{9,25},{17,1},{25,9},{2,18},{10... | collective-permute-start | bytes 442376 | tf_op jit(solution)/shard_map/ppermute | solution.py:30
  30.5 11.1 %collective-permute-start.4 = (bf16[6,32,384]{2,1,0:T(8,128)(2,1)S(1)}, bf16[6,32,384]{2,1,0:T(8,128)(2,1)S(1)}, u32[]{:S(2)}, u32[]{:S(2)}) collective-permute-start(bf16[6,32,384]{2,1,0:T(8,128)(2,1)S(1)} %collective-permute-done.3.refs_3_), channel_id=1, source_target_pairs={{0,7},{1,0},{2,1},{3,2},{4,3},{5,4},{6,5},{7,6},{8,15},{9,8},{10,9... | collective-permute-start | bytes 442376 | tf_op jit(solution)/shard_map/ppermute | solution.py:260
  31.5 12.6 %collective-permute-start.2 = (bf16[6,32,384]{2,1,0:T(8,128)(2,1)S(1)}, bf16[6,32,384]{2,1,0:T(8,128)(2,1)S(1)}, u32[]{:S(2)}, u32[]{:S(2)}) collective-permute-start(bf16[6,32,384]{2,1,0:T(8,128)(2,1)S(1)} %collective-permute-done.1.refs_2_), channel_id=1, source_target_pairs={{0,1},{1,2},{2,3},{3,4},{4,5},{5,6},{6,7},{7,0},{8,9},{9,10},{10,1... | collective-permute-start | bytes 442376 | tf_op jit(solution)/shard_map/ppermute | solution.py:262
  41.6 12.2 %copy-start = (bf16[6,32,32]{2,1,0:T(8,128)(2,1)S(1)}, bf16[6,32,32]{2,1,0:T(8,128)(2,1)}, u32[]{:S(2)}) copy-start(bf16[6,32,32]{2,1,0:T(8,128)(2,1)} %refs_9_.1) | copy-start | bytes 36868
  41.6 12.1 %collective-permute-start.5 = (bf16[6,32,384]{2,1,0:T(8,128)(2,1)S(1)}, bf16[6,32,384]{2,1,0:T(8,128)(2,1)S(1)}, u32[]{:S(2)}, u32[]{:S(2)}) collective-permute-start(bf16[6,32,384]{2,1,0:T(8,128)(2,1)S(1)} %collective-permute-done.4.refs_3_), channel_id=1, source_target_pairs={{0,7},{1,0},{2,1},{3,2},{4,3},{5,4},{6,5},{7,6},{8,15},{9,8},{10,9... | collective-permute-start | bytes 442376 | tf_op jit(solution)/shard_map/ppermute | solution.py:263
  44.0 9.7 %collective-permute-start.6 = (bf16[6,32,384]{2,1,0:T(8,128)(2,1)S(1)}, bf16[6,32,384]{2,1,0:T(8,128)(2,1)S(1)}, u32[]{:S(2)}, u32[]{:S(2)}) collective-permute-start(bf16[6,32,384]{2,1,0:T(8,128)(2,1)S(1)} %collective-permute-done.2.refs_2_), channel_id=1, source_target_pairs={{0,1},{1,2},{2,3},{3,4},{4,5},{5,6},{6,7},{7,0},{8,9},{9,10},{10,1... | collective-permute-start | bytes 442376 | tf_op jit(solution)/shard_map/ppermute | solution.py:264
  53.7 36.2 %copy-start.2 = (s32[6]{0:T(128)S(1)}, s32[6]{0:T(128)}, u32[]{:S(2)}) copy-start(s32[6]{0:T(128)} %param.9) | copy-start | bytes 76
  83.8 14.9 %all-to-all-start = ((f32[32,1,192]{2,1,0:T(1,128)}), f32[32,1,192]{2,1,0:T(1,128)S(1)}, u32[]{:S(2)}, u32[]{:S(2)}) async-start(f32[32,1,192]{2,1,0:T(1,128)} %copy.9), calls=%async_computation | async-start | bytes 65536 | tf_op jit(solution)/shard_map/all_to_all | solution.py:267
  99.3 13.3 %all-to-all-start.1 = ((f32[8,1,192]{2,1,0:T(1,128)}), f32[8,1,192]{2,1,0:T(1,128)S(1)}, u32[]{:S(2)}, u32[]{:S(2)}) async-start(f32[8,1,192]{2,1,0:T(1,128)} %broadcast_in_dim.6), calls=%async_computation.1 | async-start | bytes 16384 | tf_op jit(solution)/shard_map/all_to_all | solution.py:269

commit v4 on v3

v4 whole, which is shorter than its diff:
```python
import functools

import jax
import jax.numpy as jnp
from jax import lax
from jax.experimental import pallas as pl
from jax.experimental.pallas import tpu as pltpu
from jax.sharding import PartitionSpec as P

F32 = jnp.float32
BF16 = jnp.bfloat16
NN = (((1,), (0,)), ((), ()))
NT = (((1,), (1,)), ((), ()))
TN = (((0,), (0,)), ((), ()))
BLOCK = 8
TILE = 64
LIMIT = 24


def dot(a, b, dims):
    return lax.dot_general(a, b, dims, preferred_element_type=F32)


def shift(size, by):
    return [(i, (i + by) % size) for i in range(size)]


def column_chunks(own, rows, cols):
    pairs = [(rows * j + g, g * cols + j) for g in range(rows) for j in range(cols)]
    return lax.ppermute(own, ("grow", "gcol"), pairs)


def encode(first, partner, turn=0, mirrored=0, turned=0):
    return first + partner * 256 + (turn << 16) + (mirrored << 19) + (turned << 20) + (1 << 21)


def field(code, at, bits):
    return lax.bitwise_and(lax.shift_right_logical(code, at), (1 << bits) - 1)


def fill_table(widths, table, depth):
    at = jnp.int32(0)
    for p in range(widths.shape[0]):
        base = p * depth
        groups, rest = lax.shift_right_logical(widths[p], 3), lax.bitwise_and(widths[p], BLOCK - 1)
        few = jnp.where(rest < 5, 1, 0)

        def partner(c, at, base=base, groups=groups, few=few):
            level = lax.shift_right_logical(c, 3)
            for i in range(depth // BLOCK - 1):
                table[at + i] = encode(base + BLOCK * i, base + c, mirrored=1)
            at = at + level
            table[at] = encode(base + BLOCK * level, base + c)
            return at + jnp.where(level == groups, few, 0)

        at = lax.fori_loop(0, widths[p], partner, at)
        turned = groups + 1 - few
        for g in range(depth // BLOCK):
            for turn in range(5):
                table[at + turn] = encode(base + BLOCK * g, base + BLOCK * g, turn, int(0 < turn < 4), 1)
            at = at + jnp.where(g < turned, 5, 0)

    def clear(i, carry):
        table[at + i] = 0
        return carry

    lax.fori_loop(0, 2 * TILE, clear, 0, unroll=8)
    table[table.shape[0] - 1] = at


def partners(code, block, row):
    back = lax.bitwise_and(BLOCK - field(code, 16, 3), BLOCK - 1)
    return jnp.where(field(code, 20, 1) == 1, pltpu.roll(block, back, 0), row)


def stage_kernel(backs, opens, *refs):
    refs = list(refs)
    widths, core_ref = refs.pop(0), refs.pop(0)
    chunk_refs = [refs.pop(0) for _ in backs]
    core_v, panel, rho_a, rho_b, sems = refs[-5:]
    pairs, depth, chunk = chunk_refs[0].shape
    me = lax.axis_index("gcol")
    copies = []
    if opens:
        m_ref, table, own = refs[:3]
        copies.append(pltpu.make_async_copy(chunk_refs[0], own, sems.at[len(backs)]))
        copies[-1].start()
        chunk_refs = [own]
    else:
        table, m_ref = refs[0], refs[2 if len(refs) == 8 else 3]
    for u, back in enumerate(backs):
        rows = pl.ds(pl.multiple_of(lax.rem(me + 8 - back, 8) * chunk, chunk), chunk)
        copies.append(pltpu.make_async_copy(core_ref.at[rows], core_v.at[pl.ds(u * chunk, chunk)], sems.at[u]))
        copies[-1].start()
    if opens:
        fill_table(widths, table, depth)
        copies.pop(0).wait()
    for u in range(len(backs)):
        for p in range(pairs):
            panel[p * depth : (p + 1) * depth, u * chunk : (u + 1) * chunk] = chunk_refs[u][p].astype(F32)
    total = table[table.shape[0] - 1]

    def density(code):
        block = panel[pl.ds(pl.multiple_of(field(code, 0, 8), BLOCK), BLOCK), :]
        return block * partners(code, block, panel[pl.ds(field(code, 8, 8), 1), :])

    def build(rho, start):
        for i in range(TILE // 2):
            both = [density(table[start + 2 * i]), density(table[start + 2 * i + 1])]
            rho[16 * i : 16 * (i + 1), :] = jnp.concatenate(both, axis=0).astype(BF16)

    def multiply(rho, start, blocks):
        at = pl.ds(pl.multiple_of(start * BLOCK, 256), blocks * BLOCK)
        term = dot(rho[: blocks * BLOCK, :], core_v[...], NN)
        if opens:
            m_ref[at, :] = term
        else:
            m_ref[at, :] += term

    def step(rho, later, t):
        build(later, (t + 1) * TILE)
        multiply(rho, t * TILE, TILE)

    build(rho_a, 0)
    for copy in copies:
        copy.wait()
    tiles = (total + TILE // 2 - 1) // TILE

    def two_steps(i, carry):
        step(rho_a, rho_b, 2 * i)

        @pl.when(2 * i + 1 < tiles)
        def _():
            step(rho_b, rho_a, 2 * i + 1)

        return carry

    lax.fori_loop(0, (tiles + 1) // 2, two_steps, 0)
    odd = lax.rem(tiles, 2)
    for k, rho in enumerate((rho_a, rho_b)):

        @pl.when((total > tiles * TILE) & (odd == k))
        def _(rho=rho):
            multiply(rho, tiles * TILE, TILE // 2)


def end_kernel(widths, c0, c1, c2, c3, amps_ref, table, m_in, m_ref, out_ref, right, proj, terms, targets, acc):
    pairs, depth, chunk = c0.shape
    total = table[table.shape[0] - 1]
    for d, ref in enumerate((c0, c1, c2, c3)):
        at = pl.multiple_of(lax.rem(lax.axis_index("grow") + 4 - d, 4) * chunk, 128)
        for p in range(pairs):
            right[p * depth : (p + 1) * depth, pl.ds(at, chunk)] = ref[p]
    live = []
    for p in range(pairs):
        rows = slice(p * depth, (p + 1) * depth)
        spot = [lax.broadcasted_iota(jnp.int32, (depth, depth), k) < widths[p] for k in (0, 1)]
        live.append(spot[0] & spot[1])
        masked = jnp.where(live[p], amps_ref[p].astype(F32), 0.0).astype(BF16)
        proj[rows, :] = dot(masked, right[rows, :], NN).astype(BF16).astype(F32)
    acc[...] = jnp.zeros_like(acc)

    def finish(start, blocks):
        rows = blocks * BLOCK
        offset = lax.broadcasted_iota(jnp.int32, (BLOCK, 128), 0)

        def two(i, carry):
            plain, mirrored = [], []
            for k in range(2):
                code = table[start + 2 * i + k]
                first, partner = field(code, 0, 8), field(code, 8, 8)
                turn, turned = field(code, 16, 3), field(code, 20, 1)
                at = pl.multiple_of((start + 2 * i + k) * BLOCK, BLOCK)
                term = m_ref[pl.ds(at, BLOCK), :]
                block = proj[pl.ds(pl.multiple_of(first, BLOCK), BLOCK), :]
                plain.append(term * partners(code, block, proj[pl.ds(partner, 1), :]))
                mirrored.append(term * block)
                at = pl.multiple_of((2 * i + k) * BLOCK, BLOCK)
                targets[pl.ds(at, BLOCK), :] = offset + (first + 1024 * (field(code, 21, 1) - 1))
                over = turned * lax.bitwise_and(offset + turn, BLOCK - 1)
                targets[pl.ds(rows + at, BLOCK), :] = over + (partner + 1024 * (field(code, 19, 1) - 1))
            at = pl.multiple_of(16 * i, 16)
            terms[pl.ds(at, 16), :] = jnp.concatenate(plain, axis=0).astype(BF16)
            terms[pl.ds(rows + at, 16), :] = jnp.concatenate(mirrored, axis=0).astype(BF16)
            return carry

        lax.fori_loop(0, blocks // 2, two, 0, unroll=8)
        orbital = lax.broadcasted_iota(jnp.int32, (2 * rows, 128), 1)
        target = targets[: 2 * rows, :]
        pick = [jnp.where(target == orbital + 128 * k, 1.0, 0.0) for k in range(2)]
        pick = jnp.concatenate([pick[0], pick[1][:, : pairs * depth - 128]], axis=1).astype(BF16)
        acc[...] += dot(pick, dot(terms[: 2 * rows, :], right[...], NT).astype(BF16), TN)

    tiles = (total + TILE // 2 - 1) // TILE

    def full(t, carry):
        finish(t * TILE, TILE)
        return carry

    lax.fori_loop(0, tiles, full, 0)

    @pl.when(total > tiles * TILE)
    def _():
        finish(tiles * TILE, TILE // 2)

    for p in range(pairs):
        rows = slice(p * depth, (p + 1) * depth)
        out_ref[:, rows] = jnp.where(live[p], acc[rows, rows], 0.0)


VSPEC = pl.BlockSpec(memory_space=pltpu.VMEM)
SSPEC = pl.BlockSpec(memory_space=pltpu.SMEM)
HSPEC = pl.BlockSpec(memory_space=pltpu.HBM)


def settings(flops):
    return dict(
        cost_estimate=pl.CostEstimate(flops=flops, bytes_accessed=1 << 22, transcendentals=0),
        compiler_params=pltpu.CompilerParams(vmem_limit_bytes=LIMIT << 20),
    )


def stage(widths, core, chunks, backs, state, passed=None):
    pairs, depth, chunk = chunks[0].shape
    width = core.shape[1]
    opens = state is None
    inner = chunk * len(chunks)
    args = [widths, core, *chunks]
    specs = [SSPEC, HSPEC] + [HSPEC if opens else VSPEC] * len(chunks)
    if not opens:
        args += [state[1], state[0]]
        specs += [SSPEC, VSPEC]
    rows = pairs * depth
    groups = depth // BLOCK
    most = pairs * (BLOCK * groups * (groups - 1) // 2 + 5 * groups)
    most += -most % (TILE // 2)
    scratch = [
        pltpu.VMEM((inner, width), BF16),
        pltpu.VMEM((rows, inner), F32),
        pltpu.VMEM((TILE * BLOCK, inner), BF16),
        pltpu.VMEM((TILE * BLOCK, inner), BF16),
        pltpu.SemaphoreType.DMA((len(chunks) + 1,)),
    ]
    out, out_specs = [pltpu.VMEM((most * BLOCK, width), F32)], [VSPEC]
    aliases = {} if opens else {len(args) - 1: 0}
    if opens:
        scratch.insert(0, pltpu.VMEM((pairs, depth, chunk), BF16))
        out.append(jax.ShapeDtypeStruct((most + 3 * TILE,), jnp.int32))
        out_specs.append(SSPEC)
    if passed is not None:
        aliases[len(args)] = 1
        args.append(passed)
        specs.append(VSPEC)
        out.append(pltpu.VMEM(passed.shape, passed.dtype))
        out_specs.append(VSPEC)
    results = pl.pallas_call(
        functools.partial(stage_kernel, backs, opens),
        out_shape=out,
        in_specs=specs,
        out_specs=out_specs,
        scratch_shapes=scratch,
        input_output_aliases=aliases,
        **settings(2 * 2048 * inner * width),
    )(*args)
    return (results[0], results[1] if opens else state[1]), results[-1]


def ending(widths, columns, amplitudes, state):
    pairs, depth, chunk = columns[0].shape
    rows, width = pairs * depth, state[0].shape[1]
    return pl.pallas_call(
        end_kernel,
        out_shape=[pltpu.VMEM(state[0].shape, F32), jax.ShapeDtypeStruct((depth, rows), F32)],
        in_specs=[SSPEC] + [VSPEC] * (len(columns) + 1) + [SSPEC, VSPEC],
        out_specs=[VSPEC, VSPEC],
        scratch_shapes=[
            pltpu.VMEM((rows, width), BF16),
            pltpu.VMEM((rows, width), F32),
            pltpu.VMEM((2 * TILE * BLOCK, width), BF16),
            pltpu.VMEM((2 * TILE * BLOCK, 128), jnp.int32),
            pltpu.VMEM((rows, rows), F32),
        ],
        input_output_aliases={len(columns) + 3: 0},
        **settings(2 * 2048 * rows * width),
    )(widths, *columns, amplitudes, state[1], state[0])[1]


def local(core_matrix, pair_panels, amplitudes, pair_widths, batch_plan):
    rows, cols = lax.axis_size("grow"), lax.axis_size("gcol")
    core_matrix = pltpu.with_memory_space_constraint(core_matrix, pltpu.HBM)
    run = functools.partial(stage, pair_widths, core_matrix)
    right = lax.ppermute(pair_panels, "gcol", shift(cols, 1))
    left = lax.ppermute(pair_panels, "gcol", shift(cols, -1))
    column = column_chunks(pair_panels, rows, cols)
    state, _ = run([pltpu.with_memory_space_constraint(pair_panels, pltpu.HBM)], (0,), None)
    state, _ = run([right, left], (1, -1), state)
    right = lax.ppermute(right, "gcol", shift(cols, 1))
    left = lax.ppermute(left, "gcol", shift(cols, -1))
    state, column = run([right, left], (2, -2), state, column)
    right = lax.ppermute(right, "gcol", shift(cols, 1))
    left = lax.ppermute(left, "gcol", shift(cols, -1))
    last = lax.ppermute(right, "gcol", shift(cols, 1))
    state, _ = run([right, left, last], (3, -3, 4), state)
    columns = [column] + [lax.ppermute(column, "grow", shift(rows, d)) for d in range(1, rows)]
    parts = ending(pair_widths, columns, amplitudes, state)
    mine = lax.all_to_all(parts, ("grow", "gcol"), 0, 0, tiled=True).sum(axis=0)
    copies = jnp.broadcast_to(mine, (lax.axis_size("pair"), *mine.shape))
    every = lax.all_to_all(copies, "pair", 0, 0, tiled=True)
    every = every.reshape(-1, parts.shape[0])
    return every.at[batch_plan].get(mode="promise_in_bounds")


def solution(mesh):
    in_specs = (
        P("grow", "gcol"),
        P("pair", None, ("grow", "gcol")),
        P("pair", None, None),
        P("pair"),
        P("pair"),
    )
    out_specs = P("pair", ("grow", "gcol"))
    return jax.shard_map(local, mesh=mesh, in_specs=in_specs, out_specs=out_specs, check_vma=False)
```

time: 112 us -> 106 us (0.946); the launches traced: 114 us -> 106 us
  starting transfers between devices: 38.5 us -> 34.3 us
  Pallas kernels: 56.5 us -> 54.7 us
  waiting for transfers between devices: 15.6 us -> 14.1 us
    all_to_all x1, starting transfers between devices: 8.68 us -> 3.24 us  [local(): every = lax.all_to_all(copies, 'pair', 0, 0, tiled=True)]
    all_to_all x1, starting transfers between devices: 6.1 us -> 10.5 us  [local(): mine = lax.all_to_all(parts, ('grow', 'gcol'), 0, 0, tiled=True).sum(axis=0)]
    ppermute x3 -> x2, starting transfers between devices: 7.36 us -> 3.93 us  [local(): left = lax.ppermute(left, 'gcol', shift(cols, -1))]
    ppermute x4 -> x6, starting transfers between devices: 12.7 us -> 15 us  [the longest x3 7.05 us: local(): lax.ppermute(column, 'grow', shift(rows, d))]
    ppermute x4 -> x6, waiting for transfers between devices: 0.01 us -> 2.24 us  [the longest x1 2.22 us: local(): right = lax.ppermute(pair_panels, 'gcol', shift(cols, 1))]
    ppermute x3 -> x2, waiting for transfers between devices: 2.23 us -> 0.01 us  [local(): right = lax.ppermute(right, 'gcol', shift(cols, 1))]
    ppermute x3 -> x2, starting transfers between devices: 3.65 us -> 1.6 us  [local(): right = lax.ppermute(right, 'gcol', shift(cols, 1))]
    pallas_call x4 -> x5, Pallas kernels: 56.5 us -> 54.7 us  [the longest x4 41.2 us: stage(): pl.pallas_call(functools.partial(stage_kernel, backs, opens), out_shape=o...]
  transfers between devices with their start and end apart: 13 -> 13, of which waited for: 3 -> 3; matrix products, arithmetic and copies ran while one was open for 0% -> 0% of each run, Pallas kernels for 24% -> 39%
where the time goes in v4:
time: 106 us
  Pallas kernels  54.7 us (52%)
  starting transfers between devices  34.3 us (32%)
  waiting for transfers between devices  14.1 us (13%)
  local copies, waits for them, and re-layouts  3.11 us (3%)
    pallas_call x4, Pallas kernels, stage(): pl.pallas_call(functools.partial(stage_kernel, backs, opens), out_shape=o...  41.2 us
    pallas_call x1, Pallas kernels, ending(): pl.pallas_call(end_kernel, out_shape=[pltpu.VMEM(state[0].shape, F32), ja...  13.5 us
    all_to_all x1, starting transfers between devices, local(): mine = lax.all_to_all(parts, ('grow', 'gcol'), 0, 0, tiled=True).sum(axis=0)  10.5 us
    all_to_all x1, waiting for transfers between devices, local(): mine = lax.all_to_all(parts, ('grow', 'gcol'), 0, 0, tiled=True).sum(axis=0)  8.74 us
    ppermute x3, starting transfers between devices, local(): lax.ppermute(column, 'grow', shift(rows, d))  7.05 us
    ppermute x1, starting transfers between devices, local(): left = lax.ppermute(pair_panels, 'gcol', shift(cols, -1))  3.94 us
    ppermute x2, starting transfers between devices, local(): left = lax.ppermute(left, 'gcol', shift(cols, -1))  3.93 us
    all_to_all x1, starting transfers between devices, local(): every = lax.all_to_all(copies, 'pair', 0, 0, tiled=True)  3.24 us
  transfers between devices with their start and end apart: 13, of which 3 were waited for; matrix products, arithmetic and copies ran while one was open for 0% of the time, Pallas kernels for 39%

profile of v4, /device:TPU:1, one launch (start us, length us, event | category | flops | bytes accessed | tf_op | source)
XLA Modules:
  0.0 106.5 jit_solution(14846408220393108216)
XLA Ops:
  0.0 2.5 %collective-permute-start = (bf16[6,32,384]{2,1,0:T(8,128)(2,1)}, bf16[6,32,384]{2,1,0:T(8,128)(2,1)S(1)}, u32[]{:S(2)}, u32[]{:S(2)}) collective-permute-start(bf16[6,32,384]{2,1,0:T(8,128)(2,1)} %refs_2_.1), channel_id=1, source_target_pairs={{0,1},{1,2},{2,3},{3,4},{4,5},{5,6},{6,7},{7,0},{8,9},{9,10},{10,1... | collective-permute-start | bytes 442376 | tf_op jit(solution)/shard_map/ppermute | solution.py:292
  2.5 3.9 %collective-permute-start.2 = (bf16[6,32,384]{2,1,0:T(8,128)(2,1)}, bf16[6,32,384]{2,1,0:T(8,128)(2,1)S(1)}, u32[]{:S(2)}, u32[]{:S(2)}) collective-permute-start(bf16[6,32,384]{2,1,0:T(8,128)(2,1)} %refs_2_.1), channel_id=1, source_target_pairs={{0,7},{1,0},{2,1},{3,2},{4,3},{5,4},{6,5},{7,6},{8,15},{9,8},{10,9... | collective-permute-start | bytes 442376 | tf_op jit(solution)/shard_map/ppermute | solution.py:293
  6.4 1.6 %collective-permute-start.4 = (bf16[6,32,384]{2,1,0:T(8,128)(2,1)}, bf16[6,32,384]{2,1,0:T(8,128)(2,1)S(1)}, u32[]{:S(2)}, u32[]{:S(2)}) collective-permute-start(bf16[6,32,384]{2,1,0:T(8,128)(2,1)} %refs_2_.1), channel_id=1, source_target_pairs={{0,0},{4,1},{8,2},{12,3},{16,4},{20,5},{24,6},{28,7},{1,8},{5,9},{... | collective-permute-start | bytes 442376 | tf_op jit(solution)/shard_map/ppermute | solution.py:30
  8.0 2.2 %collective-permute-done.refs_2_ = bf16[6,32,384]{2,1,0:T(8,128)(2,1)S(1)} collective-permute-done((bf16[6,32,384]{2,1,0:T(8,128)(2,1)}, bf16[6,32,384]{2,1,0:T(8,128)(2,1)S(1)}, u32[]{:S(2)}, u32[]{:S(2)}) %collective-permute-start) | collective-permute-done | bytes 147488 | tf_op jit(solution)/shard_map/ppermute | solution.py:292
  10.2 0.7 collective-permute-start.1
  10.9 0.0 copy-start.1
  10.9 0.7 copy-done.1
  11.5 8.5 %shard_map.55 = (f32[3328,1536]{1,0:T(8,128)S(1)}, s32[608]{0:T(1024)S(1)}) custom-call(s32[6]{0:T(128)S(1)} %copy-done.1, bf16[3072,1536]{1,0:T(8,128)(2,1)} %refs_1_.7, bf16[6,32,384]{2,1,0:T(8,128)(2,1)} %refs_2_.1), custom_call_target="tpu_custom_call" | custom-call | flops 2415919104 | bytes 4194304 | tf_op jit(solution)/shard_map/pallas_call | solution.py:256
  20.0 0.0 collective-permute-done.2.refs_3_
  20.0 2.1 %collective-permute-start.3 = (bf16[6,32,384]{2,1,0:T(8,128)(2,1)S(1)}, bf16[6,32,384]{2,1,0:T(8,128)(2,1)S(1)}, u32[]{:S(2)}, u32[]{:S(2)}) collective-permute-start(bf16[6,32,384]{2,1,0:T(8,128)(2,1)S(1)} %collective-permute-done.2.refs_3_), channel_id=1, source_target_pairs={{0,7},{1,0},{2,1},{3,2},{4,3},{5,4},{6,5},{7,6},{8,15},{9,8},{10,9... | collective-permute-start | bytes 442376 | tf_op jit(solution)/shard_map/ppermute | solution.py:298
  22.1 0.0 collective-permute-done.1.refs_2_
  22.1 0.9 collective-permute-start.8
  23.0 9.4 %shard_map.56.refs_5_ = f32[3328,1536]{1,0:T(8,128)S(1)} custom-call(s32[6]{0:T(128)S(1)} %copy-done.1, bf16[3072,1536]{1,0:T(8,128)(2,1)} %refs_1_.7, bf16[6,32,384]{2,1,0:T(8,128)(2,1)S(1)} %collective-permute-done.refs_2_, bf16[6,32,384]{2,1,0:T(8,128)(2,1)S(1)} %collective-permute-done.2.refs_3_, ...), custom_call_target="tpu_custom_call", output_to_operand_aliasing={{}: (5, {})} | custom-call | flops 4831838208 | bytes 4194304 | tf_op jit(solution)/shard_map/pallas_call | solution.py:256
  32.4 0.0 collective-permute-done.3.refs_3_
  32.4 1.9 %collective-permute-start.9 = (bf16[6,32,384]{2,1,0:T(8,128)(2,1)S(1)}, bf16[6,32,384]{2,1,0:T(8,128)(2,1)S(1)}, u32[]{:S(2)}, u32[]{:S(2)}) collective-permute-start(bf16[6,32,384]{2,1,0:T(8,128)(2,1)S(1)} %collective-permute-done.3.refs_3_), channel_id=1, source_target_pairs={{0,7},{1,0},{2,1},{3,2},{4,3},{5,4},{6,5},{7,6},{8,15},{9,8},{10,9... | collective-permute-start | bytes 442376 | tf_op jit(solution)/shard_map/ppermute | solution.py:301
  34.3 0.0 collective-permute-done.8.refs_2_
  34.3 0.0 collective-permute-start.10
  34.3 0.0 collective-permute-done.4.refs_6_
  34.3 9.4 %shard_map.57 = (f32[3328,1536]{1,0:T(8,128)S(1)}, bf16[6,32,384]{2,1,0:T(8,128)(2,1)S(1)}) custom-call(s32[6]{0:T(128)S(1)} %copy-done.1, bf16[3072,1536]{1,0:T(8,128)(2,1)} %refs_1_.7, bf16[6,32,384]{2,1,0:T(8,128)(2,1)S(1)} %collective-permute-done.1.refs_2_, ...), custom_call_target="tpu_custom_call", output_to_operand_aliasing={{0}: (5, {}), {1}: (6, {})} | custom-call | flops 4831838208 | bytes 4194304 | tf_op jit(solution)/shard_map/pallas_call | solution.py:256
  43.7 2.7 %collective-permute-start.5 = (bf16[6,32,384]{2,1,0:T(8,128)(2,1)S(1)}, bf16[6,32,384]{2,1,0:T(8,128)(2,1)S(1)}, u32[]{:S(2)}, u32[]{:S(2)}) collective-permute-start(bf16[6,32,384]{2,1,0:T(8,128)(2,1)S(1)} %get-tuple-element.12.c0), channel_id=1, source_target_pairs={{0,8},{8,16},{16,24},{24,0},{1,9},{9,17},{17,25},{25,1},{2,10},{10... | collective-permute-start | bytes 442376 | tf_op jit(solution)/shard_map/ppermute | solution.py:304
  46.4 2.4 %collective-permute-start.6 = (bf16[6,32,384]{2,1,0:T(8,128)(2,1)S(1)}, bf16[6,32,384]{2,1,0:T(8,128)(2,1)S(1)}, u32[]{:S(2)}, u32[]{:S(2)}) collective-permute-start(bf16[6,32,384]{2,1,0:T(8,128)(2,1)S(1)} %get-tuple-element.12.c0), channel_id=1, source_target_pairs={{0,16},{8,24},{16,0},{24,8},{1,17},{9,25},{17,1},{25,9},{2,18},{10... | collective-permute-start | bytes 442376 | tf_op jit(solution)/shard_map/ppermute | solution.py:304
  48.8 2.0 %collective-permute-start.7 = (bf16[6,32,384]{2,1,0:T(8,128)(2,1)S(1)}, bf16[6,32,384]{2,1,0:T(8,128)(2,1)S(1)}, u32[]{:S(2)}, u32[]{:S(2)}) collective-permute-start(bf16[6,32,384]{2,1,0:T(8,128)(2,1)S(1)} %get-tuple-element.12.c0), channel_id=1, source_target_pairs={{0,24},{8,0},{16,8},{24,16},{1,25},{9,1},{17,9},{25,17},{2,26},{10... | collective-permute-start | bytes 442376 | tf_op jit(solution)/shard_map/ppermute | solution.py:304
  50.8 0.0 collective-permute-done.9.refs_3_
  50.8 0.0 collective-permute-done.10.refs_4_
  50.8 0.0 copy-start
  50.8 13.9 %shard_map.58.m_in = f32[3328,1536]{1,0:T(8,128)S(1)} custom-call(s32[6]{0:T(128)S(1)} %copy-done.1, bf16[3072,1536]{1,0:T(8,128)(2,1)} %refs_1_.7, bf16[6,32,384]{2,1,0:T(8,128)(2,1)S(1)} %collective-permute-done.8.refs_2_, bf16[6,32,384]{2,1,0:T(8,128)(2,1)S(1)} %collective-permute-done.9.refs_3_, ...), custom_call_target="tpu_custom_call", output_to_operand_aliasing={{}: (6, {})} | custom-call | flops 7247757312 | bytes 4194304 | tf_op jit(solution)/shard_map/pallas_call | solution.py:256
  64.7 0.0 copy-start.2
  64.7 0.0 collective-permute-done.5.c1
  64.8 0.0 collective-permute-done.6.c2
  64.8 0.0 collective-permute-done.7.c3
  64.8 0.0 copy-done
  64.8 13.5 %shard_map.59 = (f32[3328,1536]{1,0:T(8,128)S(1)}, f32[32,192]{1,0:T(8,128)S(1)}) custom-call(s32[6]{0:T(128)S(1)} %copy-done.1, bf16[6,32,384]{2,1,0:T(8,128)(2,1)S(1)} %get-tuple-element.12.c0, bf16[6,32,384]{2,1,0:T(8,128)(2,1)S(1)} %collective-permute-done.5.c1, ...), custom_call_target="tpu_custom_call", output_to_operand_aliasing={{0}: (7, {})} | custom-call | flops 1207959552 | bytes 4194304 | tf_op jit(solution)/shard_map/pallas_call | solution.py:271
  78.2 0.6 copy.11
  78.9 10.5 %all-to-all-start = ((f32[32,1,192]{2,1,0:T(1,128)}), f32[32,1,192]{2,1,0:T(1,128)S(1)}, u32[]{:S(2)}, u32[]{:S(2)}) async-start(f32[32,1,192]{2,1,0:T(1,128)} %copy.11), calls=%async_computation | async-start | bytes 65536 | tf_op jit(solution)/shard_map/all_to_all | solution.py:306
  89.4 0.0 copy-done.2
  89.4 8.7 %all-to-all-done = f32[32,1,192]{2,1,0:T(1,128)S(1)} async-done(((f32[32,1,192]{2,1,0:T(1,128)}), f32[32,1,192]{2,1,0:T(1,128)S(1)}, u32[]{:S(2)}, u32[]{:S(2)}) %all-to-all-start) | async-done | bytes 24608 | tf_op jit(solution)/shard_map/all_to_all | solution.py:306
  98.2 0.1 reduce_sum.9
  98.2 0.6 broadcast_in_dim.6
  98.8 3.2 %all-to-all-start.1 = ((f32[8,1,192]{2,1,0:T(1,128)}), f32[8,1,192]{2,1,0:T(1,128)S(1)}, u32[]{:S(2)}, u32[]{:S(2)}) async-start(f32[8,1,192]{2,1,0:T(1,128)} %broadcast_in_dim.6), calls=%async_computation.1 | async-start | bytes 16384 | tf_op jit(solution)/shard_map/all_to_all | solution.py:308
  102.1 3.1 %all-to-all-done.1 = f32[8,1,192]{2,1,0:T(1,128)S(1)} async-done(((f32[8,1,192]{2,1,0:T(1,128)}), f32[8,1,192]{2,1,0:T(1,128)S(1)}, u32[]{:S(2)}, u32[]{:S(2)}) %all-to-all-start.1) | async-done | bytes 6176 | tf_op jit(solution)/shard_map/all_to_all | solution.py:308
  105.3 0.1 reshape.10
  105.3 1.1 %gather_fusion = f32[6,32]{1,0:T(8,128)} fusion(f32[48,32]{1,0:T(8,128)S(1)} %reshape.10, s32[1024]{0:T(1024)S(1)} %pad_clamp_fusion), kind=kCustom, calls=%fused_computation | custom fusion | bytes 1560 | tf_op jit(solution)/shard_map/gather | solution.py:310
  (3 shorter events, 0.0 us)
Async XLA Ops:
  0.0 10.2 %collective-permute-start = (bf16[6,32,384]{2,1,0:T(8,128)(2,1)}, bf16[6,32,384]{2,1,0:T(8,128)(2,1)S(1)}, u32[]{:S(2)}, u32[]{:S(2)}) collective-permute-start(bf16[6,32,384]{2,1,0:T(8,128)(2,1)} %refs_2_.1), channel_id=1, source_target_pairs={{0,1},{1,2},{2,3},{3,4},{4,5},{5,6},{6,7},{7,0},{8,9},{9,10},{10,1... | collective-permute-start | bytes 442376 | tf_op jit(solution)/shard_map/ppermute | solution.py:292
  2.5 17.5 %collective-permute-start.2 = (bf16[6,32,384]{2,1,0:T(8,128)(2,1)}, bf16[6,32,384]{2,1,0:T(8,128)(2,1)S(1)}, u32[]{:S(2)}, u32[]{:S(2)}) collective-permute-start(bf16[6,32,384]{2,1,0:T(8,128)(2,1)} %refs_2_.1), channel_id=1, source_target_pairs={{0,7},{1,0},{2,1},{3,2},{4,3},{5,4},{6,5},{7,6},{8,15},{9,8},{10,9... | collective-permute-start | bytes 442376 | tf_op jit(solution)/shard_map/ppermute | solution.py:293
  6.4 27.9 %collective-permute-start.4 = (bf16[6,32,384]{2,1,0:T(8,128)(2,1)}, bf16[6,32,384]{2,1,0:T(8,128)(2,1)S(1)}, u32[]{:S(2)}, u32[]{:S(2)}) collective-permute-start(bf16[6,32,384]{2,1,0:T(8,128)(2,1)} %refs_2_.1), channel_id=1, source_target_pairs={{0,0},{4,1},{8,2},{12,3},{16,4},{20,5},{24,6},{28,7},{1,8},{5,9},{... | collective-permute-start | bytes 442376 | tf_op jit(solution)/shard_map/ppermute | solution.py:30
  10.2 11.9 %collective-permute-start.1 = (bf16[6,32,384]{2,1,0:T(8,128)(2,1)S(1)}, bf16[6,32,384]{2,1,0:T(8,128)(2,1)S(1)}, u32[]{:S(2)}, u32[]{:S(2)}) collective-permute-start(bf16[6,32,384]{2,1,0:T(8,128)(2,1)S(1)} %collective-permute-done.refs_2_), channel_id=1, source_target_pairs={{0,1},{1,2},{2,3},{3,4},{4,5},{5,6},{6,7},{7,0},{8,9},{9,10},{10,1... | collective-permute-start | bytes 442376 | tf_op jit(solution)/shard_map/ppermute | solution.py:297
  10.9 0.7 copy-start.1
  20.0 12.4 %collective-permute-start.3 = (bf16[6,32,384]{2,1,0:T(8,128)(2,1)S(1)}, bf16[6,32,384]{2,1,0:T(8,128)(2,1)S(1)}, u32[]{:S(2)}, u32[]{:S(2)}) collective-permute-start(bf16[6,32,384]{2,1,0:T(8,128)(2,1)S(1)} %collective-permute-done.2.refs_3_), channel_id=1, source_target_pairs={{0,7},{1,0},{2,1},{3,2},{4,3},{5,4},{6,5},{7,6},{8,15},{9,8},{10,9... | collective-permute-start | bytes 442376 | tf_op jit(solution)/shard_map/ppermute | solution.py:298
  22.1 12.2 %collective-permute-start.8 = (bf16[6,32,384]{2,1,0:T(8,128)(2,1)S(1)}, bf16[6,32,384]{2,1,0:T(8,128)(2,1)S(1)}, u32[]{:S(2)}, u32[]{:S(2)}) collective-permute-start(bf16[6,32,384]{2,1,0:T(8,128)(2,1)S(1)} %collective-permute-done.1.refs_2_), channel_id=1, source_target_pairs={{0,1},{1,2},{2,3},{3,4},{4,5},{5,6},{6,7},{7,0},{8,9},{9,10},{10,1... | collective-permute-start | bytes 442376 | tf_op jit(solution)/shard_map/ppermute | solution.py:300
  32.4 18.4 %collective-permute-start.9 = (bf16[6,32,384]{2,1,0:T(8,128)(2,1)S(1)}, bf16[6,32,384]{2,1,0:T(8,128)(2,1)S(1)}, u32[]{:S(2)}, u32[]{:S(2)}) collective-permute-start(bf16[6,32,384]{2,1,0:T(8,128)(2,1)S(1)} %collective-permute-done.3.refs_3_), channel_id=1, source_target_pairs={{0,7},{1,0},{2,1},{3,2},{4,3},{5,4},{6,5},{7,6},{8,15},{9,8},{10,9... | collective-permute-start | bytes 442376 | tf_op jit(solution)/shard_map/ppermute | solution.py:301
  34.3 16.5 %collective-permute-start.10 = (bf16[6,32,384]{2,1,0:T(8,128)(2,1)S(1)}, bf16[6,32,384]{2,1,0:T(8,128)(2,1)S(1)}, u32[]{:S(2)}, u32[]{:S(2)}) collective-permute-start(bf16[6,32,384]{2,1,0:T(8,128)(2,1)S(1)} %collective-permute-done.8.refs_2_), channel_id=1, source_target_pairs={{0,1},{1,2},{2,3},{3,4},{4,5},{5,6},{6,7},{7,0},{8,9},{9,10},{10,1... | collective-permute-start | bytes 442376 | tf_op jit(solution)/shard_map/ppermute | solution.py:302
  43.7 21.0 %collective-permute-start.5 = (bf16[6,32,384]{2,1,0:T(8,128)(2,1)S(1)}, bf16[6,32,384]{2,1,0:T(8,128)(2,1)S(1)}, u32[]{:S(2)}, u32[]{:S(2)}) collective-permute-start(bf16[6,32,384]{2,1,0:T(8,128)(2,1)S(1)} %get-tuple-element.12.c0), channel_id=1, source_target_pairs={{0,8},{8,16},{16,24},{24,0},{1,9},{9,17},{17,25},{25,1},{2,10},{10... | collective-permute-start | bytes 442376 | tf_op jit(solution)/shard_map/ppermute | solution.py:304
  46.4 18.4 %collective-permute-start.6 = (bf16[6,32,384]{2,1,0:T(8,128)(2,1)S(1)}, bf16[6,32,384]{2,1,0:T(8,128)(2,1)S(1)}, u32[]{:S(2)}, u32[]{:S(2)}) collective-permute-start(bf16[6,32,384]{2,1,0:T(8,128)(2,1)S(1)} %get-tuple-element.12.c0), channel_id=1, source_target_pairs={{0,16},{8,24},{16,0},{24,8},{1,17},{9,25},{17,1},{25,9},{2,18},{10... | collective-permute-start | bytes 442376 | tf_op jit(solution)/shard_map/ppermute | solution.py:304
  48.8 16.0 %collective-permute-start.7 = (bf16[6,32,384]{2,1,0:T(8,128)(2,1)S(1)}, bf16[6,32,384]{2,1,0:T(8,128)(2,1)S(1)}, u32[]{:S(2)}, u32[]{:S(2)}) collective-permute-start(bf16[6,32,384]{2,1,0:T(8,128)(2,1)S(1)} %get-tuple-element.12.c0), channel_id=1, source_target_pairs={{0,24},{8,0},{16,8},{24,16},{1,25},{9,1},{17,9},{25,17},{2,26},{10... | collective-permute-start | bytes 442376 | tf_op jit(solution)/shard_map/ppermute | solution.py:304
  50.8 14.0 %copy-start = (bf16[6,32,32]{2,1,0:T(8,128)(2,1)S(1)}, bf16[6,32,32]{2,1,0:T(8,128)(2,1)}, u32[]{:S(2)}) copy-start(bf16[6,32,32]{2,1,0:T(8,128)(2,1)} %amps_ref.1) | copy-start | bytes 36868
  64.7 24.7 %copy-start.2 = (s32[6]{0:T(128)S(1)}, s32[6]{0:T(128)}, u32[]{:S(2)}) copy-start(s32[6]{0:T(128)} %param.9) | copy-start | bytes 76
  78.9 19.3 %all-to-all-start = ((f32[32,1,192]{2,1,0:T(1,128)}), f32[32,1,192]{2,1,0:T(1,128)S(1)}, u32[]{:S(2)}, u32[]{:S(2)}) async-start(f32[32,1,192]{2,1,0:T(1,128)} %copy.11), calls=%async_computation | async-start | bytes 65536 | tf_op jit(solution)/shard_map/all_to_all | solution.py:306
  98.8 6.4 %all-to-all-start.1 = ((f32[8,1,192]{2,1,0:T(1,128)}), f32[8,1,192]{2,1,0:T(1,128)S(1)}, u32[]{:S(2)}, u32[]{:S(2)}) async-start(f32[8,1,192]{2,1,0:T(1,128)} %broadcast_in_dim.6), calls=%async_computation.1 | async-start | bytes 16384 | tf_op jit(solution)/shard_map/all_to_all | solution.py:308

commit v5 on v4

--- a/solution.py
+++ b/solution.py
@@ -144,9 +144,8 @@
             multiply(rho, tiles * TILE, TILE // 2)
 
 
-def end_kernel(widths, c0, c1, c2, c3, amps_ref, table, m_in, m_ref, out_ref, right, proj, terms, targets, acc):
+def end_kernel(widths, c0, c1, c2, c3, amps_ref, m_in, m_ref, out_ref, right, proj, plain, mirror):
     pairs, depth, chunk = c0.shape
-    total = table[table.shape[0] - 1]
     for d, ref in enumerate((c0, c1, c2, c3)):
         at = pl.multiple_of(lax.rem(lax.axis_index("grow") + 4 - d, 4) * chunk, 128)
         for p in range(pairs):
@@ -158,54 +157,87 @@
         live.append(spot[0] & spot[1])
         masked = jnp.where(live[p], amps_ref[p].astype(F32), 0.0).astype(BF16)
         proj[rows, :] = dot(masked, right[rows, :], NN).astype(BF16).astype(F32)
-    acc[...] = jnp.zeros_like(acc)
-
-    def finish(start, blocks):
-        rows = blocks * BLOCK
-        offset = lax.broadcasted_iota(jnp.int32, (BLOCK, 128), 0)
-
-        def two(i, carry):
-            plain, mirrored = [], []
-            for k in range(2):
-                code = table[start + 2 * i + k]
-                first, partner = field(code, 0, 8), field(code, 8, 8)
-                turn, turned = field(code, 16, 3), field(code, 20, 1)
-                at = pl.multiple_of((start + 2 * i + k) * BLOCK, BLOCK)
-                term = m_ref[pl.ds(at, BLOCK), :]
-                block = proj[pl.ds(pl.multiple_of(first, BLOCK), BLOCK), :]
-                plain.append(term * partners(code, block, proj[pl.ds(partner, 1), :]))
-                mirrored.append(term * block)
-                at = pl.multiple_of((2 * i + k) * BLOCK, BLOCK)
-                targets[pl.ds(at, BLOCK), :] = offset + (first + 1024 * (field(code, 21, 1) - 1))
-                over = turned * lax.bitwise_and(offset + turn, BLOCK - 1)
-                targets[pl.ds(rows + at, BLOCK), :] = over + (partner + 1024 * (field(code, 19, 1) - 1))
-            at = pl.multiple_of(16 * i, 16)
-            terms[pl.ds(at, 16), :] = jnp.concatenate(plain, axis=0).astype(BF16)
-            terms[pl.ds(rows + at, 16), :] = jnp.concatenate(mirrored, axis=0).astype(BF16)
+    plain[...] = jnp.zeros_like(plain)
+    mirror[...] = jnp.zeros_like(mirror)
+    half = plain.shape[1] // 2
+
+    def group_rows(base, group):
+        return pl.ds(pl.multiple_of(base + BLOCK * group, BLOCK), BLOCK)
+
+    def term_rows(at):
+        return pl.ds(pl.multiple_of(at * BLOCK, BLOCK), BLOCK)
+
+    def spread(base, start, level, live_here, own, cols):
+        blocks = level + own
+
+        def partner(k, sums):
+            c = base + BLOCK * level + k
+            row = proj[pl.ds(c, 1), cols]
+            sums, back = list(sums), None
+            for i in range(blocks):
+                term = m_ref[term_rows(start + k * blocks + i), cols]
+                sums[i] = sums[i] + term * row
+                if i < level:
+                    image = term * proj[group_rows(base, i), cols]
+                    back = image if back is None else back + image
+            if level:
+                mirror[pl.ds(c, 1), cols] = jnp.sum(back, axis=0, keepdims=True)
+            return tuple(sums)
+
+        unroll = 4 if isinstance(live_here, int) else 1
+        sums = lax.fori_loop(0, live_here, partner, (jnp.zeros((BLOCK, half), F32),) * blocks, unroll=unroll)
+        for i in range(blocks):
+            plain[group_rows(base, i), cols] += sums[i]
+
+    def turn_group(base, start, group, cols):
+        block = proj[group_rows(base, group), cols]
+        total = None
+        for turn in range(5):
+            term = m_ref[term_rows(start + turn), cols]
+            ahead = pltpu.roll(block, BLOCK - turn, 0) if turn else block
+            total = term * ahead if total is None else total + term * ahead
+            if 0 < turn < 4:
+                total = total + pltpu.roll(term * block, turn, 0)
+        plain[group_rows(base, group), cols] += total
+
+    def pair_sums(p, at):
+        base = p * depth
+        groups, rest = lax.shift_right_logical(widths[p], 3), lax.bitwise_and(widths[p], BLOCK - 1)
+        few = jnp.where(rest < 5, 1, 0)
+        for level in range(depth // BLOCK):
+            here = jnp.clip(widths[p] - BLOCK * level, 0, BLOCK)
+            extra = jnp.where(groups == level, few, 0)
+            for own in range(2):
+                if level + own:
+
+                    @pl.when((extra == own) & (here > 0) & (here < BLOCK))
+                    def _(at=at, level=level, here=here, own=own):
+                        for h in range(2):
+                            spread(base, at, level, here, own, slice(h * half, (h + 1) * half))
+
+            if level:
+
+                @pl.when(here == BLOCK)
+                def _(at=at, level=level):
+                    for h in range(2):
+                        spread(base, at, level, BLOCK, 0, slice(h * half, (h + 1) * half))
+
+            at = at + here * (level + extra)
+        turned = groups + 1 - few
+
+        def turns(g, carry):
+            for h in range(2):
+                turn_group(base, at + 5 * g, g, slice(h * half, (h + 1) * half))
             return carry
 
-        lax.fori_loop(0, blocks // 2, two, 0, unroll=8)
-        orbital = lax.broadcasted_iota(jnp.int32, (2 * rows, 128), 1)
-        target = targets[: 2 * rows, :]
-        pick = [jnp.where(target == orbital + 128 * k, 1.0, 0.0) for k in range(2)]
-        pick = jnp.concatenate([pick[0], pick[1][:, : pairs * depth - 128]], axis=1).astype(BF16)
-        acc[...] += dot(pick, dot(terms[: 2 * rows, :], right[...], NT).astype(BF16), TN)
-
-    tiles = (total + TILE // 2 - 1) // TILE
-
-    def full(t, carry):
-        finish(t * TILE, TILE)
-        return carry
-
-    lax.fori_loop(0, tiles, full, 0)
-
-    @pl.when(total > tiles * TILE)
-    def _():
-        finish(tiles * TILE, TILE // 2)
-
+        lax.fori_loop(0, turned, turns, 0)
+        return at + 5 * turned
+
+    lax.fori_loop(0, pairs, pair_sums, jnp.int32(0))
     for p in range(pairs):
         rows = slice(p * depth, (p + 1) * depth)
-        out_ref[:, rows] = jnp.where(live[p], acc[rows, rows], 0.0)
+        both = (plain[rows, :] + mirror[rows, :]).astype(BF16)
+        out_ref[:, rows] = jnp.where(live[p], dot(both, right[rows, :], NT), 0.0)
 
 
 VSPEC = pl.BlockSpec(memory_space=pltpu.VMEM)
@@ -271,18 +303,17 @@
     return pl.pallas_call(
         end_kernel,
         out_shape=[pltpu.VMEM(state[0].shape, F32), jax.ShapeDtypeStruct((depth, rows), F32)],
-        in_specs=[SSPEC] + [VSPEC] * (len(columns) + 1) + [SSPEC, VSPEC],
+        in_specs=[SSPEC] + [VSPEC] * (len(columns) + 2),
         out_specs=[VSPEC, VSPEC],
         scratch_shapes=[
             pltpu.VMEM((rows, width), BF16),
             pltpu.VMEM((rows, width), F32),
-            pltpu.VMEM((2 * TILE * BLOCK, width), BF16),
-            pltpu.VMEM((2 * TILE * BLOCK, 128), jnp.int32),
-            pltpu.VMEM((rows, rows), F32),
+            pltpu.VMEM((rows, width), F32),
+            pltpu.VMEM((rows, width), F32),
         ],
-        input_output_aliases={len(columns) + 3: 0},
+        input_output_aliases={len(columns) + 2: 0},
         **settings(2 * 2048 * rows * width),
-    )(widths, *columns, amplitudes, state[1], state[0])[1]
+    )(widths, *columns, amplitudes, state[0])[1]
 
 
 def local(core_matrix, pair_panels, amplitudes, pair_widths, batch_plan):

time: 106 us -> 102 us (0.962); the launches traced: 106 us -> 100 us
  Pallas kernels: 54.7 us -> 33.7 us
  starting transfers between devices: 34.3 us -> 46.6 us
  waiting for transfers between devices: 14.1 us -> 16.7 us
    pallas_call x4, Pallas kernels: 41.2 us -> 28.8 us  [stage(): pl.pallas_call(functools.partial(stage_kernel, backs, opens), out_shape=o...]
    all_to_all x1, starting transfers between devices: 3.24 us -> 14.1 us  [local(): every = lax.all_to_all(copies, 'pair', 0, 0, tiled=True)]
    pallas_call x1, Pallas kernels: 13.5 us -> 4.95 us  [ending(): pl.pallas_call(end_kernel, out_shape=[pltpu.VMEM(state[0].shape, F32), ja...]
    all_to_all x1, waiting for transfers between devices: 3.14 us -> 4.61 us  [local(): every = lax.all_to_all(copies, 'pair', 0, 0, tiled=True)]
    ppermute x2, starting transfers between devices: 3.93 us -> 2.61 us  [local(): left = lax.ppermute(left, 'gcol', shift(cols, -1))]
    ppermute x2, starting transfers between devices: 1.6 us -> 2.89 us  [local(): right = lax.ppermute(right, 'gcol', shift(cols, 1))]
    all_to_all x1, starting transfers between devices: 10.5 us -> 11.7 us  [local(): mine = lax.all_to_all(parts, ('grow', 'gcol'), 0, 0, tiled=True).sum(axis=0)]
    ppermute x2, waiting for transfers between devices: 0.01 us -> 1.07 us  [local(): right = lax.ppermute(right, 'gcol', shift(cols, 1))]
  transfers between devices with their start and end apart: 13 -> 13, of which waited for: 3 -> 4; matrix products, arithmetic and copies ran while one was open for 0% -> 0% of each run, Pallas kernels for 39% -> 29%
where the time goes in v5:
time: 102 us; the launch traced here: 100 us
  starting transfers between devices  46.6 us (46%)
  Pallas kernels  33.7 us (33%)
  waiting for transfers between devices  16.7 us (16%)
  local copies, waits for them, and re-layouts  3.12 us (3%)
    pallas_call x4, Pallas kernels, stage(): pl.pallas_call(functools.partial(stage_kernel, backs, opens), out_shape=o...  28.8 us
    all_to_all x1, starting transfers between devices, local(): every = lax.all_to_all(copies, 'pair', 0, 0, tiled=True)  14.1 us
    all_to_all x1, starting transfers between devices, local(): mine = lax.all_to_all(parts, ('grow', 'gcol'), 0, 0, tiled=True).sum(axis=0)  11.7 us
    all_to_all x1, waiting for transfers between devices, local(): mine = lax.all_to_all(parts, ('grow', 'gcol'), 0, 0, tiled=True).sum(axis=0)  8.82 us
    ppermute x3, starting transfers between devices, local(): lax.ppermute(column, 'grow', shift(rows, d))  6.33 us
    pallas_call x1, Pallas kernels, ending(): pl.pallas_call(end_kernel, out_shape=[pltpu.VMEM(state[0].shape, F32), ja...  4.95 us
    all_to_all x1, waiting for transfers between devices, local(): every = lax.all_to_all(copies, 'pair', 0, 0, tiled=True)  4.61 us
    ppermute x1, starting transfers between devices, local(): left = lax.ppermute(pair_panels, 'gcol', shift(cols, -1))  3.94 us
  transfers between devices with their start and end apart: 13, of which 4 were waited for; matrix products, arithmetic and copies ran while one was open for 0% of the time, Pallas kernels for 29%

profile of v5, /device:TPU:1, one launch (start us, length us, event | category | flops | bytes accessed | tf_op | source)
XLA Modules:
  0.0 100.4 jit_solution(3457768495528216504)
XLA Ops:
  0.0 2.5 %collective-permute-start = (bf16[6,32,384]{2,1,0:T(8,128)(2,1)}, bf16[6,32,384]{2,1,0:T(8,128)(2,1)S(1)}, u32[]{:S(2)}, u32[]{:S(2)}) collective-permute-start(bf16[6,32,384]{2,1,0:T(8,128)(2,1)} %refs_2_.1), channel_id=1, source_target_pairs={{0,1},{1,2},{2,3},{3,4},{4,5},{5,6},{6,7},{7,0},{8,9},{9,10},{10,1... | collective-permute-start | bytes 442376 | tf_op jit(solution)/shard_map/ppermute | solution.py:323
  2.5 3.9 %collective-permute-start.2 = (bf16[6,32,384]{2,1,0:T(8,128)(2,1)}, bf16[6,32,384]{2,1,0:T(8,128)(2,1)S(1)}, u32[]{:S(2)}, u32[]{:S(2)}) collective-permute-start(bf16[6,32,384]{2,1,0:T(8,128)(2,1)} %refs_2_.1), channel_id=1, source_target_pairs={{0,7},{1,0},{2,1},{3,2},{4,3},{5,4},{6,5},{7,6},{8,15},{9,8},{10,9... | collective-permute-start | bytes 442376 | tf_op jit(solution)/shard_map/ppermute | solution.py:324
  6.4 1.6 %collective-permute-start.4 = (bf16[6,32,384]{2,1,0:T(8,128)(2,1)}, bf16[6,32,384]{2,1,0:T(8,128)(2,1)S(1)}, u32[]{:S(2)}, u32[]{:S(2)}) collective-permute-start(bf16[6,32,384]{2,1,0:T(8,128)(2,1)} %refs_2_.1), channel_id=1, source_target_pairs={{0,0},{4,1},{8,2},{12,3},{16,4},{20,5},{24,6},{28,7},{1,8},{5,9},{... | collective-permute-start | bytes 442376 | tf_op jit(solution)/shard_map/ppermute | solution.py:30
  8.0 2.2 %collective-permute-done.refs_2_ = bf16[6,32,384]{2,1,0:T(8,128)(2,1)S(1)} collective-permute-done((bf16[6,32,384]{2,1,0:T(8,128)(2,1)}, bf16[6,32,384]{2,1,0:T(8,128)(2,1)S(1)}, u32[]{:S(2)}, u32[]{:S(2)}) %collective-permute-start) | collective-permute-done | bytes 147488 | tf_op jit(solution)/shard_map/ppermute | solution.py:323
  10.2 0.7 collective-permute-start.1
  10.9 0.0 copy-start.1
  10.9 0.7 copy-done.1
  11.5 6.0 %shard_map.55 = (f32[3328,1536]{1,0:T(8,128)S(1)}, s32[608]{0:T(1024)S(1)}) custom-call(s32[6]{0:T(128)S(1)} %copy-done.1, bf16[3072,1536]{1,0:T(8,128)(2,1)} %refs_1_.7, bf16[6,32,384]{2,1,0:T(8,128)(2,1)} %refs_2_.1), custom_call_target="tpu_custom_call" | custom-call | flops 2415919104 | bytes 4194304 | tf_op jit(solution)/shard_map/pallas_call | solution.py:288
  17.5 0.0 collective-permute-done.2.refs_3_
  17.5 2.1 %collective-permute-start.3 = (bf16[6,32,384]{2,1,0:T(8,128)(2,1)S(1)}, bf16[6,32,384]{2,1,0:T(8,128)(2,1)S(1)}, u32[]{:S(2)}, u32[]{:S(2)}) collective-permute-start(bf16[6,32,384]{2,1,0:T(8,128)(2,1)S(1)} %collective-permute-done.2.refs_3_), channel_id=1, source_target_pairs={{0,7},{1,0},{2,1},{3,2},{4,3},{5,4},{6,5},{7,6},{8,15},{9,8},{10,9... | collective-permute-start | bytes 442376 | tf_op jit(solution)/shard_map/ppermute | solution.py:329
  19.6 1.1 %collective-permute-done.1.refs_2_ = bf16[6,32,384]{2,1,0:T(8,128)(2,1)S(1)} collective-permute-done((bf16[6,32,384]{2,1,0:T(8,128)(2,1)S(1)}, bf16[6,32,384]{2,1,0:T(8,128)(2,1)S(1)}, u32[]{:S(2)}, u32[]{:S(2)}) %collective-permute-start.1) | collective-permute-done | bytes 147488 | tf_op jit(solution)/shard_map/ppermute | solution.py:328
  20.7 2.2 %collective-permute-start.8 = (bf16[6,32,384]{2,1,0:T(8,128)(2,1)S(1)}, bf16[6,32,384]{2,1,0:T(8,128)(2,1)S(1)}, u32[]{:S(2)}, u32[]{:S(2)}) collective-permute-start(bf16[6,32,384]{2,1,0:T(8,128)(2,1)S(1)} %collective-permute-done.1.refs_2_), channel_id=1, source_target_pairs={{0,1},{1,2},{2,3},{3,4},{4,5},{5,6},{6,7},{7,0},{8,9},{9,10},{10,1... | collective-permute-start | bytes 442376 | tf_op jit(solution)/shard_map/ppermute | solution.py:331
  22.9 6.6 %shard_map.56.refs_5_ = f32[3328,1536]{1,0:T(8,128)S(1)} custom-call(s32[6]{0:T(128)S(1)} %copy-done.1, bf16[3072,1536]{1,0:T(8,128)(2,1)} %refs_1_.7, bf16[6,32,384]{2,1,0:T(8,128)(2,1)S(1)} %collective-permute-done.refs_2_, bf16[6,32,384]{2,1,0:T(8,128)(2,1)S(1)} %collective-permute-done.2.refs_3_, ...), custom_call_target="tpu_custom_call", output_to_operand_aliasing={{}: (5, {})} | custom-call | flops 4831838208 | bytes 4194304 | tf_op jit(solution)/shard_map/pallas_call | solution.py:288
  29.4 0.0 collective-permute-done.3.refs_3_
  29.5 0.5 collective-permute-start.9
  30.0 0.0 collective-permute-done.8.refs_2_
  30.0 1.0 collective-permute-start.10
  31.0 0.0 collective-permute-done.4.refs_6_
  31.0 6.6 %shard_map.57 = (f32[3328,1536]{1,0:T(8,128)S(1)}, bf16[6,32,384]{2,1,0:T(8,128)(2,1)S(1)}) custom-call(s32[6]{0:T(128)S(1)} %copy-done.1, bf16[3072,1536]{1,0:T(8,128)(2,1)} %refs_1_.7, bf16[6,32,384]{2,1,0:T(8,128)(2,1)S(1)} %collective-permute-done.1.refs_2_, ...), custom_call_target="tpu_custom_call", output_to_operand_aliasing={{0}: (5, {}), {1}: (6, {})} | custom-call | flops 4831838208 | bytes 4194304 | tf_op jit(solution)/shard_map/pallas_call | solution.py:288
  37.6 0.6 collective-permute-start.5
  38.2 3.8 %collective-permute-start.6 = (bf16[6,32,384]{2,1,0:T(8,128)(2,1)S(1)}, bf16[6,32,384]{2,1,0:T(8,128)(2,1)S(1)}, u32[]{:S(2)}, u32[]{:S(2)}) collective-permute-start(bf16[6,32,384]{2,1,0:T(8,128)(2,1)S(1)} %get-tuple-element.12.c0), channel_id=1, source_target_pairs={{0,16},{8,24},{16,0},{24,8},{1,17},{9,25},{17,1},{25,9},{2,18},{10... | collective-permute-start | bytes 442376 | tf_op jit(solution)/shard_map/ppermute | solution.py:335
  42.0 2.0 %collective-permute-start.7 = (bf16[6,32,384]{2,1,0:T(8,128)(2,1)S(1)}, bf16[6,32,384]{2,1,0:T(8,128)(2,1)S(1)}, u32[]{:S(2)}, u32[]{:S(2)}) collective-permute-start(bf16[6,32,384]{2,1,0:T(8,128)(2,1)S(1)} %get-tuple-element.12.c0), channel_id=1, source_target_pairs={{0,24},{8,0},{16,8},{24,16},{1,25},{9,1},{17,9},{25,17},{2,26},{10... | collective-permute-start | bytes 442376 | tf_op jit(solution)/shard_map/ppermute | solution.py:335
  43.9 0.0 collective-permute-done.9.refs_3_
  43.9 0.0 collective-permute-done.10.refs_4_
  43.9 0.0 copy-start
  44.0 9.6 %shard_map.58.m_in = f32[3328,1536]{1,0:T(8,128)S(1)} custom-call(s32[6]{0:T(128)S(1)} %copy-done.1, bf16[3072,1536]{1,0:T(8,128)(2,1)} %refs_1_.7, bf16[6,32,384]{2,1,0:T(8,128)(2,1)S(1)} %collective-permute-done.8.refs_2_, bf16[6,32,384]{2,1,0:T(8,128)(2,1)S(1)} %collective-permute-done.9.refs_3_, ...), custom_call_target="tpu_custom_call", output_to_operand_aliasing={{}: (6, {})} | custom-call | flops 7247757312 | bytes 4194304 | tf_op jit(solution)/shard_map/pallas_call | solution.py:288
  53.6 0.0 copy-start.2
  53.6 0.0 collective-permute-done.5.c1
  53.6 0.0 collective-permute-done.6.c2
  53.6 0.0 collective-permute-done.7.c3
  53.7 0.0 copy-done
  53.7 5.0 %shard_map.59 = (f32[3328,1536]{1,0:T(8,128)S(1)}, f32[32,192]{1,0:T(8,128)S(1)}) custom-call(s32[6]{0:T(128)S(1)} %copy-done.1, bf16[6,32,384]{2,1,0:T(8,128)(2,1)S(1)} %get-tuple-element.12.c0, bf16[6,32,384]{2,1,0:T(8,128)(2,1)S(1)} %collective-permute-done.5.c1, ...), custom_call_target="tpu_custom_call", output_to_operand_aliasing={{0}: (6, {})} | custom-call | flops 1207959552 | bytes 4194304 | tf_op jit(solution)/shard_map/pallas_call | solution.py:303
  58.6 0.6 copy.11
  59.3 11.7 %all-to-all-start = ((f32[32,1,192]{2,1,0:T(1,128)}), f32[32,1,192]{2,1,0:T(1,128)S(1)}, u32[]{:S(2)}, u32[]{:S(2)}) async-start(f32[32,1,192]{2,1,0:T(1,128)} %copy.11), calls=%async_computation | async-start | bytes 65536 | tf_op jit(solution)/shard_map/all_to_all | solution.py:337
  71.0 0.0 copy-done.2
  71.0 8.8 %all-to-all-done = f32[32,1,192]{2,1,0:T(1,128)S(1)} async-done(((f32[32,1,192]{2,1,0:T(1,128)}), f32[32,1,192]{2,1,0:T(1,128)S(1)}, u32[]{:S(2)}, u32[]{:S(2)}) %all-to-all-start) | async-done | bytes 24608 | tf_op jit(solution)/shard_map/all_to_all | solution.py:337
  79.8 0.1 reduce_sum.9
  79.9 0.6 broadcast_in_dim.6
  80.5 14.1 %all-to-all-start.1 = ((f32[8,1,192]{2,1,0:T(1,128)}), f32[8,1,192]{2,1,0:T(1,128)S(1)}, u32[]{:S(2)}, u32[]{:S(2)}) async-start(f32[8,1,192]{2,1,0:T(1,128)} %broadcast_in_dim.6), calls=%async_computation.1 | async-start | bytes 16384 | tf_op jit(solution)/shard_map/all_to_all | solution.py:339
  94.6 4.6 %all-to-all-done.1 = f32[8,1,192]{2,1,0:T(1,128)S(1)} async-done(((f32[8,1,192]{2,1,0:T(1,128)}), f32[8,1,192]{2,1,0:T(1,128)S(1)}, u32[]{:S(2)}, u32[]{:S(2)}) %all-to-all-start.1) | async-done | bytes 6176 | tf_op jit(solution)/shard_map/all_to_all | solution.py:339
  99.2 0.1 reshape.10
  99.3 1.1 %gather_fusion = f32[6,32]{1,0:T(8,128)} fusion(f32[48,32]{1,0:T(8,128)S(1)} %reshape.10, s32[1024]{0:T(1024)S(1)} %pad_clamp_fusion), kind=kCustom, calls=%fused_computation | custom fusion | bytes 1560 | tf_op jit(solution)/shard_map/gather | solution.py:341
  (3 shorter events, 0.0 us)
Async XLA Ops:
  0.0 10.2 %collective-permute-start = (bf16[6,32,384]{2,1,0:T(8,128)(2,1)}, bf16[6,32,384]{2,1,0:T(8,128)(2,1)S(1)}, u32[]{:S(2)}, u32[]{:S(2)}) collective-permute-start(bf16[6,32,384]{2,1,0:T(8,128)(2,1)} %refs_2_.1), channel_id=1, source_target_pairs={{0,1},{1,2},{2,3},{3,4},{4,5},{5,6},{6,7},{7,0},{8,9},{9,10},{10,1... | collective-permute-start | bytes 442376 | tf_op jit(solution)/shard_map/ppermute | solution.py:323
  2.5 15.0 %collective-permute-start.2 = (bf16[6,32,384]{2,1,0:T(8,128)(2,1)}, bf16[6,32,384]{2,1,0:T(8,128)(2,1)S(1)}, u32[]{:S(2)}, u32[]{:S(2)}) collective-permute-start(bf16[6,32,384]{2,1,0:T(8,128)(2,1)} %refs_2_.1), channel_id=1, source_target_pairs={{0,7},{1,0},{2,1},{3,2},{4,3},{5,4},{6,5},{7,6},{8,15},{9,8},{10,9... | collective-permute-start | bytes 442376 | tf_op jit(solution)/shard_map/ppermute | solution.py:324
  6.4 24.6 %collective-permute-start.4 = (bf16[6,32,384]{2,1,0:T(8,128)(2,1)}, bf16[6,32,384]{2,1,0:T(8,128)(2,1)S(1)}, u32[]{:S(2)}, u32[]{:S(2)}) collective-permute-start(bf16[6,32,384]{2,1,0:T(8,128)(2,1)} %refs_2_.1), channel_id=1, source_target_pairs={{0,0},{4,1},{8,2},{12,3},{16,4},{20,5},{24,6},{28,7},{1,8},{5,9},{... | collective-permute-start | bytes 442376 | tf_op jit(solution)/shard_map/ppermute | solution.py:30
  10.2 10.5 %collective-permute-start.1 = (bf16[6,32,384]{2,1,0:T(8,128)(2,1)S(1)}, bf16[6,32,384]{2,1,0:T(8,128)(2,1)S(1)}, u32[]{:S(2)}, u32[]{:S(2)}) collective-permute-start(bf16[6,32,384]{2,1,0:T(8,128)(2,1)S(1)} %collective-permute-done.refs_2_), channel_id=1, source_target_pairs={{0,1},{1,2},{2,3},{3,4},{4,5},{5,6},{6,7},{7,0},{8,9},{9,10},{10,1... | collective-permute-start | bytes 442376 | tf_op jit(solution)/shard_map/ppermute | solution.py:328
  10.9 0.7 copy-start.1
  17.5 11.9 %collective-permute-start.3 = (bf16[6,32,384]{2,1,0:T(8,128)(2,1)S(1)}, bf16[6,32,384]{2,1,0:T(8,128)(2,1)S(1)}, u32[]{:S(2)}, u32[]{:S(2)}) collective-permute-start(bf16[6,32,384]{2,1,0:T(8,128)(2,1)S(1)} %collective-permute-done.2.refs_3_), channel_id=1, source_target_pairs={{0,7},{1,0},{2,1},{3,2},{4,3},{5,4},{6,5},{7,6},{8,15},{9,8},{10,9... | collective-permute-start | bytes 442376 | tf_op jit(solution)/shard_map/ppermute | solution.py:329
  20.7 9.4 %collective-permute-start.8 = (bf16[6,32,384]{2,1,0:T(8,128)(2,1)S(1)}, bf16[6,32,384]{2,1,0:T(8,128)(2,1)S(1)}, u32[]{:S(2)}, u32[]{:S(2)}) collective-permute-start(bf16[6,32,384]{2,1,0:T(8,128)(2,1)S(1)} %collective-permute-done.1.refs_2_), channel_id=1, source_target_pairs={{0,1},{1,2},{2,3},{3,4},{4,5},{5,6},{6,7},{7,0},{8,9},{9,10},{10,1... | collective-permute-start | bytes 442376 | tf_op jit(solution)/shard_map/ppermute | solution.py:331
  29.5 14.5 %collective-permute-start.9 = (bf16[6,32,384]{2,1,0:T(8,128)(2,1)S(1)}, bf16[6,32,384]{2,1,0:T(8,128)(2,1)S(1)}, u32[]{:S(2)}, u32[]{:S(2)}) collective-permute-start(bf16[6,32,384]{2,1,0:T(8,128)(2,1)S(1)} %collective-permute-done.3.refs_3_), channel_id=1, source_target_pairs={{0,7},{1,0},{2,1},{3,2},{4,3},{5,4},{6,5},{7,6},{8,15},{9,8},{10,9... | collective-permute-start | bytes 442376 | tf_op jit(solution)/shard_map/ppermute | solution.py:332
  30.0 13.9 %collective-permute-start.10 = (bf16[6,32,384]{2,1,0:T(8,128)(2,1)S(1)}, bf16[6,32,384]{2,1,0:T(8,128)(2,1)S(1)}, u32[]{:S(2)}, u32[]{:S(2)}) collective-permute-start(bf16[6,32,384]{2,1,0:T(8,128)(2,1)S(1)} %collective-permute-done.8.refs_2_), channel_id=1, source_target_pairs={{0,1},{1,2},{2,3},{3,4},{4,5},{5,6},{6,7},{7,0},{8,9},{9,10},{10,1... | collective-permute-start | bytes 442376 | tf_op jit(solution)/shard_map/ppermute | solution.py:333
  37.6 16.0 %collective-permute-start.5 = (bf16[6,32,384]{2,1,0:T(8,128)(2,1)S(1)}, bf16[6,32,384]{2,1,0:T(8,128)(2,1)S(1)}, u32[]{:S(2)}, u32[]{:S(2)}) collective-permute-start(bf16[6,32,384]{2,1,0:T(8,128)(2,1)S(1)} %get-tuple-element.12.c0), channel_id=1, source_target_pairs={{0,8},{8,16},{16,24},{24,0},{1,9},{9,17},{17,25},{25,1},{2,10},{10... | collective-permute-start | bytes 442376 | tf_op jit(solution)/shard_map/ppermute | solution.py:335
  38.2 15.4 %collective-permute-start.6 = (bf16[6,32,384]{2,1,0:T(8,128)(2,1)S(1)}, bf16[6,32,384]{2,1,0:T(8,128)(2,1)S(1)}, u32[]{:S(2)}, u32[]{:S(2)}) collective-permute-start(bf16[6,32,384]{2,1,0:T(8,128)(2,1)S(1)} %get-tuple-element.12.c0), channel_id=1, source_target_pairs={{0,16},{8,24},{16,0},{24,8},{1,17},{9,25},{17,1},{25,9},{2,18},{10... | collective-permute-start | bytes 442376 | tf_op jit(solution)/shard_map/ppermute | solution.py:335
  42.0 11.7 %collective-permute-start.7 = (bf16[6,32,384]{2,1,0:T(8,128)(2,1)S(1)}, bf16[6,32,384]{2,1,0:T(8,128)(2,1)S(1)}, u32[]{:S(2)}, u32[]{:S(2)}) collective-permute-start(bf16[6,32,384]{2,1,0:T(8,128)(2,1)S(1)} %get-tuple-element.12.c0), channel_id=1, source_target_pairs={{0,24},{8,0},{16,8},{24,16},{1,25},{9,1},{17,9},{25,17},{2,26},{10... | collective-permute-start | bytes 442376 | tf_op jit(solution)/shard_map/ppermute | solution.py:335
  43.9 9.7 %copy-start = (bf16[6,32,32]{2,1,0:T(8,128)(2,1)S(1)}, bf16[6,32,32]{2,1,0:T(8,128)(2,1)}, u32[]{:S(2)}) copy-start(bf16[6,32,32]{2,1,0:T(8,128)(2,1)} %amps_ref.1) | copy-start | bytes 36868
  53.6 17.4 %copy-start.2 = (s32[6]{0:T(128)S(1)}, s32[6]{0:T(128)}, u32[]{:S(2)}) copy-start(s32[6]{0:T(128)} %param.9) | copy-start | bytes 76
  59.3 20.6 %all-to-all-start = ((f32[32,1,192]{2,1,0:T(1,128)}), f32[32,1,192]{2,1,0:T(1,128)S(1)}, u32[]{:S(2)}, u32[]{:S(2)}) async-start(f32[32,1,192]{2,1,0:T(1,128)} %copy.11), calls=%async_computation | async-start | bytes 65536 | tf_op jit(solution)/shard_map/all_to_all | solution.py:337
  80.5 18.7 %all-to-all-start.1 = ((f32[8,1,192]{2,1,0:T(1,128)}), f32[8,1,192]{2,1,0:T(1,128)S(1)}, u32[]{:S(2)}, u32[]{:S(2)}) async-start(f32[8,1,192]{2,1,0:T(1,128)} %broadcast_in_dim.6), calls=%async_computation.1 | async-start | bytes 16384 | tf_op jit(solution)/shard_map/all_to_all | solution.py:339
